TPU v7x, 32 devices: a whole 2x2x4 slice. The times are simulated.
32 devices in a mesh: groups: 2 (over y), ctx: 4 (over z), tp: 2 (over x), dp: 2 (over core).
Axes of the slice: x: 2, y: 2, z: 4, core: 2. Of those that a mesh axis runs over, the one named last changes fastest.
Arguments:
- x_in: bfloat16 [4096, 8192], P(('groups', 'ctx', 'dp'), 'tp'), parts along dimension 0, may hold values from -6 to 6
- bc_in: bfloat16 [4096, 2, 1024], P(('groups', 'ctx', 'dp'), None, 'tp'), parts along dimension 0, may hold values from -6 to 6
- gate_z: bfloat16 [4096, 8192], P(('groups', 'ctx', 'dp'), 'tp'), parts along dimension 0, may hold values from -60 to 60
- log_decay: float32 [2, 4096, 128], P(None, ('groups', 'ctx', 'dp'), 'tp'), parts along dimension 1, may hold values from -1 to 0
- resets: int32 [4096], P(('groups', 'ctx', 'dp')), parts along dimension 0, may hold values from 0 to 1, as said below
- conv_x: float32 [4, 8192], P(None, 'tp'), may hold values from -3 to 3
- conv_bc: float32 [4, 2, 1024], P(None, None, 'tp'), may hold values from -1.8 to 1.8
- skip_d: float32 [128], P('tp'), may hold values from 0.25 to 2
- norm_gain: float32 [8192], P('tp'), may hold values from 0.5 to 1.5
- visit_span: int32 [256, 2], P(('groups', 'ctx', 'dp')), parts along dimension 0, may hold values from 0 to 2048, as said below
Outputs:
- token_out: bfloat16 [4096, 8192], P(('groups', 'ctx', 'dp'), 'tp'), parts along dimension 0
- pooled: bfloat16 [256, 8192], P(('groups', 'ctx', 'dp'), 'tp'), parts along dimension 0
There are 2 independent parts, one for each index of `groups`. A program takes and returns all parts, laid end to end along the dimension named above; an argument that names none is the same for every part. Nothing has to cross between parts.
Inputs may be any that keep to these rules, and one draw needn't show every extreme that they name: `resets`: at most 3 tokens carry a 1, never token 0; a 1 opens a new patient stream. `visit_span`: the visits in rows k * 16 to (k + 1) * 16 - 1 begin in tokens k * 256 to (k + 1) * 256 - 1; every visit holds 1 to 256 tokens and some visit holds exactly 256; visits may intersect.
All inputs are finite; a program needn't handle non-finite values.
Results may differ from a plain program's by a relative error of at most 0.0036.
Values may be sent and summed in bfloat16 or wider, within the bound.
A program may use at most 128 MiB of HBM per device.

v0:
```python
import jax
import jax.numpy as jnp
from jax import lax
from jax.sharding import PartitionSpec as P

HEADDIM = 64
STATE = 128
GROUPS = 8
INNER = 8192
STRETCH = 256


def from_behind(block, axis, distance):
    devices = range(lax.axis_size(axis))
    route = [(i - distance, i) for i in devices if i - distance in devices]
    return lax.ppermute(block, axis, route)


def carried_in(x, axis, combine, identity, reverse):
    peers, mine = (lax.axis_size(axis), lax.axis_index(axis))
    everything = jax.tree.map(lambda part: lax.all_gather(part, axis), x)
    start = jax.tree.map(
        lambda part, zero: jnp.broadcast_to(jnp.asarray(zero, part.dtype), part.shape), x, identity
    )

    def lap(k, before):
        at = peers - 1 - k if reverse else k
        reached = at > mine if reverse else at < mine
        new = combine(before, jax.tree.map(lambda part: part[at], everything))
        return jax.tree.map(lambda a, b: jnp.where(reached, a, b), new, before)

    return lax.fori_loop(0, peers, lap, start)


def conv_silu(signal, rim, weight):
    kernel = weight.shape[0]
    length = signal.shape[0]
    padded = jnp.concatenate([rim, signal], axis=0).astype(jnp.float32)
    summed = weight[0] * padded[0:length]
    for offset in range(1, kernel):
        summed = summed + weight[offset] * padded[offset : offset + length]
    return jax.nn.silu(summed).astype(jnp.bfloat16)


def input_weight(log_rate):
    return jnp.sqrt(-jnp.expm1(2.0 * log_rate))


def stretch_parts(x_block, b_block, c_block, log_block, break_block, scale_block, strict):
    length = x_block.shape[0]
    per_group = x_block.shape[1] // b_block.shape[1]
    cumul = jnp.cumsum(log_block, axis=0)
    segment = jnp.cumsum(break_block)
    token_position = jnp.arange(length)
    if strict:
        ordered = token_position[:, None] > token_position[None, :]
    else:
        ordered = token_position[:, None] >= token_position[None, :]
    keeping = (ordered & (segment[:, None] == segment[None, :]))[None]
    cumul_t = cumul.T
    spread = jnp.where(keeping, cumul_t[:, :, None] - cumul_t[:, None, :], 0.0)
    decays = jnp.where(keeping, jnp.exp(spread), 0.0)
    scores = jnp.einsum("ign,jgn->gij", c_block, b_block, preferred_element_type=jnp.float32)
    scores = jnp.repeat(scores, per_group, axis=0)
    mixing = (scores * decays * scale_block.T[:, None, :]).astype(jnp.bfloat16)
    y_inner = jnp.einsum("hij,jhp->ihp", mixing, x_block, preferred_element_type=jnp.float32)
    same_end = (segment[-1] == segment).astype(jnp.float32)
    to_end = jnp.exp(cumul[-1][None, :] - cumul) * same_end[:, None] * scale_block
    weighted = (x_block.astype(jnp.float32) * to_end[:, :, None]).astype(jnp.bfloat16)
    b_heads = jnp.repeat(b_block, per_group, axis=1)
    stretch_state = jnp.einsum(
        "jhp,jhn->hpn", weighted, b_heads, preferred_element_type=jnp.float32
    )
    carried = jnp.exp(cumul[-1]) * (segment[-1] == 0).astype(jnp.float32)
    leading = jnp.exp(cumul) * (segment == 0).astype(jnp.float32)[:, None]
    return (y_inner, stretch_state, carried, leading)


def local_parts(x_heads, b_mat, c_mat, log_rate, break_flags, scales, strict):
    stretches = x_heads.shape[0] // STRETCH

    def blocks(array):
        return array.reshape((stretches, STRETCH) + array.shape[1:])

    def one_block(pieces):
        return stretch_parts(*pieces, strict)

    return lax.map(
        one_block,
        tuple((blocks(a) for a in (x_heads, b_mat, c_mat, log_rate, break_flags, scales))),
    )


def carry_chain(stretch_states, carries, start_state):

    def advance(state_now, pieces):
        return (pieces[1][:, None, None] * state_now + pieces[0], state_now)

    return lax.scan(advance, start_state, (stretch_states, carries))


def combine(earlier, later):
    return (earlier[0] * later[0], later[0][:, None, None] * earlier[1] + later[1])


def finish(parts, c_mat, incoming):
    y_inner, stretch_states, carries, leading = parts
    stretches = carries.shape[0]
    heads_here = carries.shape[1]
    per_group = heads_here // c_mat.shape[1]
    c_heads = jnp.repeat(c_mat, per_group, axis=1).astype(jnp.float32)
    c_heads = c_heads.reshape((stretches, STRETCH) + c_heads.shape[1:])
    _, seeded = carry_chain(stretch_states, carries, incoming)
    from_state = leading[..., None] * jnp.einsum(
        "cihn,chpn->cihp", c_heads, seeded, precision=lax.Precision.HIGHEST
    )
    summed = y_inner + from_state
    return summed.reshape((stretches * STRETCH,) + summed.shape[2:])


def on_device(
    x_in, bc_in, gate_z, log_decay, resets, conv_x, conv_bc, skip_d, norm_gain, visit_span
):
    kernel = conv_x.shape[0]
    tokens_here = x_in.shape[0]
    rim_x, rim_bc = from_behind(
        (x_in[tokens_here - kernel + 1 :], bc_in[tokens_here - kernel + 1 :]), ("ctx", "dp"), 1
    )
    x_conv = conv_silu(x_in, rim_x, conv_x)
    bc_conv = conv_silu(bc_in, rim_bc, conv_bc)
    heads_here = log_decay.shape[2]
    groups_here = bc_in.shape[2] // STATE
    x_heads = x_conv.reshape(tokens_here, heads_here, HEADDIM)
    b_mat = bc_conv[:, 0].reshape(tokens_here, groups_here, STATE)
    c_mat = bc_conv[:, 1].reshape(tokens_here, groups_here, STATE)
    forward_log = log_decay[0]
    backward_log = log_decay[1]
    fwd_parts = local_parts(
        x_heads, b_mat, c_mat, forward_log, resets, input_weight(forward_log), False
    )
    rev_log = jnp.concatenate(
        [jnp.zeros((1, heads_here), jnp.float32), jnp.flip(backward_log, 0)[:-1]], axis=0
    )
    rev_break = jnp.concatenate([jnp.zeros((1,), jnp.int32), jnp.flip(resets, 0)[:-1]], axis=0)
    c_rev = jnp.flip(c_mat, 0)
    bwd_parts = local_parts(
        jnp.flip(x_heads, 0),
        jnp.flip(b_mat, 0),
        c_rev,
        rev_log,
        rev_break,
        jnp.flip(input_weight(backward_log), 0),
        True,
    )
    zero_state = jnp.zeros((heads_here, HEADDIM, STATE), jnp.float32)
    fwd_end, fwd_enter = carry_chain(fwd_parts[1], fwd_parts[2], zero_state)
    bwd_end, bwd_enter = carry_chain(bwd_parts[1], bwd_parts[2], zero_state)
    fwd_total = jnp.prod(fwd_parts[2], axis=0)
    post_factor = jnp.exp(backward_log[0]) * (1 - resets[0]).astype(jnp.float32)
    bwd_total = jnp.prod(bwd_parts[2], axis=0) * post_factor
    bwd_end = bwd_end * post_factor[:, None, None]
    identity = (jnp.ones((heads_here,), jnp.float32), zero_state)
    fwd_in = carried_in((fwd_total, fwd_end), ("ctx", "dp"), combine, identity, False)[1]
    bwd_in = carried_in((bwd_total, bwd_end), ("ctx", "dp"), combine, identity, True)[1]
    fwd_y = finish(fwd_parts, c_mat, fwd_in)
    bwd_y = jnp.flip(finish(bwd_parts, c_rev, bwd_in), 0)
    mixed = fwd_y + bwd_y + skip_d[None, :, None] * x_heads.astype(jnp.float32)
    group_width = INNER // GROUPS
    gated = mixed.reshape(tokens_here, groups_here, group_width) * jax.nn.silu(
        gate_z.astype(jnp.float32)
    ).reshape(tokens_here, groups_here, group_width)
    mean_sq = jnp.mean(gated * gated, axis=2, keepdims=True)
    normed = (gated * lax.rsqrt(mean_sq + 1e-05)).reshape(
        tokens_here, groups_here * group_width
    ) * norm_gain
    token_out = normed.astype(jnp.bfloat16)
    offset_here = lax.axis_index(("ctx", "dp")) * tokens_here

    def visit_sums_for(spans):
        token_position = offset_here + jnp.arange(tokens_here)
        inside = (
            (token_position[None, :] >= spans[:, 0:1]) & (token_position[None, :] < spans[:, 1:2])
        ).astype(jnp.bfloat16)
        sums = jnp.dot(inside, token_out, preferred_element_type=jnp.float32)
        return sums / jnp.maximum(spans[:, 1:2] - spans[:, 0:1], 1).astype(jnp.float32)

    earlier_spans = from_behind(visit_span, ("ctx", "dp"), 1)
    spill = visit_sums_for(earlier_spans)
    returned = from_behind(spill, ("ctx", "dp"), -1)
    pooled = (visit_sums_for(visit_span) + returned).astype(jnp.bfloat16)
    return (token_out, pooled)


def solution(mesh):
    return jax.shard_map(
        on_device,
        mesh=mesh,
        in_specs=(
            P(("groups", "ctx", "dp"), "tp"),
            P(("groups", "ctx", "dp"), None, "tp"),
            P(("groups", "ctx", "dp"), "tp"),
            P(None, ("groups", "ctx", "dp"), "tp"),
            P(("groups", "ctx", "dp")),
            P(None, "tp"),
            P(None, None, "tp"),
            P("tp"),
            P("tp"),
            P(("groups", "ctx", "dp"), None),
        ),
        out_specs=(P(("groups", "ctx", "dp"), "tp"), P(("groups", "ctx", "dp"), "tp")),
        check_vma=False,
    )
```

profile of v0, /device:TPU:1, one launch (start us, length us, event | category | flops | bytes accessed | tf_op | source)
XLA Modules:
  0.0 423.5 jit_solution(3132064480502935936)
XLA Ops:
  8.8 4.6 %collective-permute-start.1 = (bf16[3,2,512]{0,2,1:T(8,128)(2,1)}, bf16[3,2,512]{0,2,1:T(8,128)(2,1)S(1)}, u32[]{:S(2)}, u32[]{:S(2)}) collective-permute-start(bf16[3,2,512]{0,2,1:T(8,128)(2,1)} %copy.79), channel_id=1, source_target_pairs={{0,1},{1,4},{4,5},{5,8},{8,9},{9,12},{12,13},{2,3},{3,6},{6,7},{7,... | collective-permute-start | bytes 18440 | tf_op jit(solution)/shard_map/ppermute | solution.py:16
  36.7 3.5 multiply_convert_fusion.2
  40.2 3.3 copy.78
  43.5 4.2 rev.22
  59.2 3.7 collective-permute-start.2
  63.7 9.3 %all-gather.3 = f32[8,1,64]{2,1,0:T(1,128)S(1)} all-gather(f32[1,1,64]{2,1,0:T(1,128)S(1)} %copy-done.26), channel_id=1, replica_groups=mesh['groups'=2,'ctx'=4,'tp'=2,'dp'=2] {'ctx','dp'}, dimensions={0}, use_global_device_ids=true | all-gather | bytes 2304 | tf_op jit(solution)/shard_map/all_gather | solution.py:21
  73.0 14.9 %all-gather.2 = f32[8,1,64]{2,1,0:T(1,128)S(1)} all-gather(f32[1,1,64]{2,1,0:T(1,128)S(1)} %bitcast.238), channel_id=1, replica_groups=mesh['groups'=2,'ctx'=4,'tp'=2,'dp'=2] {'ctx','dp'}, dimensions={0}, use_global_device_ids=true | all-gather | bytes 2304 | tf_op jit(solution)/shard_map/all_gather | solution.py:21
  89.3 4.8 %convert_multiply_fusion = f32[256,4096]{1,0:T(8,128)} fusion(bf16[256,4096]{1,0:T(8,128)(2,1)} %param.16), kind=kLoop, calls=%fused_computation.12 | loop fusion | flops 5242880 | bytes 6291456 | tf_op jit(solution)/shard_map/jit(silu)/mul | solution.py:169
  94.8 5.6 %copy.99 = f32[256,4096]{0,1:T(8,128)} copy(f32[256,4096]{1,0:T(8,128)} %convert_multiply_fusion) | data formatting | bytes 8388608 | tf_op jit(solution)/shard_map/jit(silu)/mul | solution.py:169
  103.3 6.3 %fusion.3 = bf16[64,256,256]{2,1,0:T(8,128)(2,1)S(1)} fusion(f32[64,256]{1,0:T(8,128)} %copy.92, f32[64,256]{1,0:T(8,128)S(1)} %copy_bitcast_fusion, f32[4,256,256]{2,1,0:T(8,128)S(1)} %fusion.56, pred[256,256]{1,0:T(8,128)(4,1)} %fusion.33), kind=kLoop, calls=%fused_computation.8 | loop fusion | flops 25165824 | bytes 9633792 | tf_op jit(solution)/shard_map/while/body/eval_jaxpr/convert_element_type | solution.py:65
  110.0 6.3 %fusion.5 = bf16[64,256,256]{2,1,0:T(8,128)(2,1)} fusion(f32[64,256]{1,0:T(8,128)S(1)} %copy-done.14, f32[64,256]{1,0:T(8,128)S(1)} %get-tuple-element.423, f32[4,256,256]{2,1,0:T(8,128)S(1)} %fusion.54, pred[256,256]{1,0:T(8,128)(4,1)S(1)} %copy-done.12), kind=kLoop, calls=%fused_computation.11 | loop fusion | flops 25165824 | bytes 9633792 | tf_op jit(solution)/shard_map/while/body/eval_jaxpr/convert_element_type | solution.py:65
  116.3 4.6 %fusion.57 = f32[64,64,256]{2,1,0:T(8,128)} fusion(bf16[256,64,64]{0,2,1:T(8,128)(2,1)S(1)} %copy-done.4, bf16[64,256,256]{2,1,0:T(8,128)(2,1)S(1)} %fusion.3), kind=kOutput, calls=%fused_computation.132 | convolution fusion | flops 536870912 | bytes 14680064 | tf_op jit(solution)/shard_map/while/body/eval_jaxpr/hij,jhp->ihp/dot_general | solution.py:66
  120.8 82.4 %all-gather.9.cloned.1.call-done = f32[512,64,128]{2,1,0:T(8,128)} async-done(((f32[64,64,128]{2,1,0:T(8,128)}), f32[512,64,128]{2,1,0:T(8,128)}) %all-gather.9.cloned.1.call-update) | async-done | bytes 16777232 | tf_op jit(solution)/shard_map/all_gather | solution.py:21
  203.2 31.7 %while.21 = (s32[]{:T(128)}, f32[64,64,128]{2,1,0:T(8,128)}, s32[]{:T(128)}, f32[8,64]{1,0:T(8,128)S(1)}, f32[8,64,64,128]{3,2,1,0:T(8,128)}, /*index=5*/s32[]{:T(128)}, s32[]{:T(128)}, s32[]{:T(128)}, s32[]{:T(128)}) while((s32[]{:T(128)}, f32[64,64,128]{2,1,0:T(8,128)}, s32[]{:T(128)}, f32[8,64]{1,0:T(8,128)S(1)}, ...), condition=%wide.region_11.12_spmd.clone, body=%wide.region_10.11_spmd.clone.sunk | while | flops 2097160 | bytes 6292391 | solution.py:32
  203.2 3.3 fusion.77
  206.5 3.8 fusion.77
  210.4 4.5 %fusion.77 = f32[64,64,128]{2,1,0:T(8,128)} fusion(f32[8,64,64,128]{3,2,1,0:T(8,128)} %get-tuple-element.525, s32[]{:T(128)S(6)} %select_n.96, f32[64,64,128]{2,1,0:T(8,128)} %get-tuple-element.513, f32[64]{0:T(128)S(1)} %dynamic-slice_bitcast_fusion.5, pred[]{:T(512)S(6)} %compare.8, pred[]{:T(512)S(6)} %gt.36), kind=kLoop, calls=%fused_computation.4.clone.1 | loop fusion | flops 2097152 | bytes 6291718 | tf_op jit(solution)/shard_map/while/body/eval_jaxpr/jit(_where)/select_n | solution.py:30
  214.9 4.5 %fusion.77 = f32[64,64,128]{2,1,0:T(8,128)} fusion(f32[8,64,64,128]{3,2,1,0:T(8,128)} %get-tuple-element.525, s32[]{:T(128)S(6)} %select_n.96, f32[64,64,128]{2,1,0:T(8,128)} %get-tuple-element.513, f32[64]{0:T(128)S(1)} %dynamic-slice_bitcast_fusion.5, pred[]{:T(512)S(6)} %compare.8, pred[]{:T(512)S(6)} %gt.36), kind=kLoop, calls=%fused_computation.4.clone.1 | loop fusion | flops 2097152 | bytes 6291718 | tf_op jit(solution)/shard_map/while/body/eval_jaxpr/jit(_where)/select_n | solution.py:30
  219.4 3.8 fusion.77
  223.2 3.9 fusion.77
  227.1 3.8 fusion.77
  230.9 4.0 fusion.77
  236.5 7.6 %fusion.17 = f32[256,64,64]{0,2,1:T(8,128)} fusion(f32[64,64,256]{2,1,0:T(8,128)} %fusion.57, f32[64,64,128]{2,1,0:T(8,128)S(1)} %copy-done, bf16[256,64,128]{2,0,1:T(8,128)(2,1)S(1)} %bitcast.210, f32[256,64]{0,1:T(8,128)S(1)} %copy-done.11), kind=kOutput, calls=%fused_computation.34 | convolution fusion | flops 1612709888 | bytes 14745600 | tf_op jit(solution)/shard_map/cihn,chpn->cihp/dot_general | solution.py:114
  244.1 7.3 %rev.26 = f32[256,64,64]{0,2,1:T(8,128)} reverse(f32[256,64,64]{0,2,1:T(8,128)} %fusion.17), dimensions={0} | reverse | bytes 8388608 | tf_op jit(solution)/shard_map/jit(_flip)/rev | solution.py:166
  251.4 102.8 %all-gather.7.cloned.1.call-done = f32[512,64,128]{2,1,0:T(8,128)} async-done(((f32[64,64,128]{2,1,0:T(8,128)}), f32[512,64,128]{2,1,0:T(8,128)}) %all-gather.7.cloned.1.call-update) | async-done | bytes 16777232 | tf_op jit(solution)/shard_map/all_gather | solution.py:21
  354.2 16.9 %while.20 = (s32[]{:T(128)}, f32[64,64,128]{2,1,0:T(8,128)S(1)}, s32[]{:T(128)}, f32[8,64]{1,0:T(8,128)S(1)}, f32[8,64,64,128]{3,2,1,0:T(8,128)}, /*index=5*/s32[]{:T(128)}, s32[]{:T(128)}) while((s32[]{:T(128)}, f32[64,64,128]{2,1,0:T(8,128)S(1)}, s32[]{:T(128)}, f32[8,64]{1,0:T(8,128)S(1)}, f32[8,64,64,128]{3,2,1,0:T(8,128)}, ...), condition=%wide.region_5.6_spmd.clone, body=%wide.region_4.5_spmd.clone.sunk | while | flops 2097156 | bytes 6292329 | solution.py:32
  372.2 6.0 %fusion.55 = f32[64,64,256]{2,1,0:T(8,128)} fusion(f32[64,64,128]{2,1,0:T(8,128)S(1)} %get-tuple-element.348, bf16[256,64,128]{2,0,1:T(8,128)(2,1)S(1)} %bitcast.214), kind=kOutput, calls=%fused_computation.130 | convolution fusion | flops 1610612736 | bytes 10485760 | tf_op jit(solution)/shard_map/cihn,chpn->cihp/dot_general | solution.py:114
  378.2 11.8 %multiply_reduce_fusion = (f32[256,64]{0,1:T(8,128)S(1)}, f32[256,64,64]{0,2,1:T(8,128)}) fusion(f32[256,4096]{0,1:T(8,128)} %copy.99, bf16[256,64,64]{0,2,1:T(8,128)(2,1)S(1)} %bitcast.209, f32[64]{0:T(128)S(1)} %copy-done.29, f32[256,64,64]{0,2,1:T(8,128)} %rev.26, f32[64,64,256]{2,1,0:T(8,128)} %fusion.55, f32[256,64]{0,1:T(8,128)S(1)} %copy-done.13, ...), kind=kOutput, calls=%fused_computation.40 | convolution fusion | flops 546291712 | bytes 27394304 | tf_op jit(solution)/shard_map/while/body/eval_jaxpr/hij,jhp->ihp/dot_general | solution.py:66
  390.8 5.7 %copy.110 = f32[32,8,4,1024]{3,1,2,0:T(8,128)} copy(f32[32,8,4,1024]{3,2,1,0:T(4,128)S(1)} %bitcast.215) | data formatting | bytes 8388608
  396.6 5.8 %copy.98 = f32[256,4096]{1,0:T(8,128)} copy(f32[256,4096]{0,1:T(8,128)} %bitcast.216) | data formatting | bytes 8388608 | tf_op jit(solution)/shard_map/reshape | solution.py:169
  402.4 5.0 %multiply_convert_fusion = bf16[256,4096]{1,0:T(8,128)(2,1)S(1)} fusion(f32[256,4096]{1,0:T(8,128)} %bitcast.212, f32[256,4096]{1,0:T(8,128)} %copy.98, f32[4096]{0:T(1024)S(1)} %copy-done.18, bf16[256,4096]{1,0:T(8,128)(2,1)S(1)} %copy-done.6), kind=kLoop, calls=%fused_computation.39 | loop fusion | flops 9437184 | bytes 12599296 | tf_op jit(solution)/shard_map/convert_element_type | solution.py:176
  410.0 5.5 %collective-permute-done.3 = f32[16,4096]{1,0:T(8,128)S(1)} collective-permute-done((f32[16,4096]{1,0:T(8,128)S(1)}, f32[16,4096]{1,0:T(8,128)S(1)}, u32[]{:S(2)}, u32[]{:S(2)}) %collective-permute-start.3) | collective-permute-done | bytes 262176 | tf_op jit(solution)/shard_map/ppermute | solution.py:16
  (181 shorter events, 64.0 us)
Async XLA Ops:
  7.2 196.1 %all-gather.9.cloned.1.call-start = ((), (), s32[]{:S(2)}) async-start(), calls=%async_computation.1 | async-start | bytes 18874368 | tf_op jit(solution)/shard_map/all_gather | solution.py:21
  8.8 23.4 %collective-permute-start.1 = (bf16[3,2,512]{0,2,1:T(8,128)(2,1)}, bf16[3,2,512]{0,2,1:T(8,128)(2,1)S(1)}, u32[]{:S(2)}, u32[]{:S(2)}) collective-permute-start(bf16[3,2,512]{0,2,1:T(8,128)(2,1)} %copy.79), channel_id=1, source_target_pairs={{0,1},{1,4},{4,5},{5,8},{8,9},{9,12},{12,13},{2,3},{3,6},{6,7},{7,... | collective-permute-start | bytes 18440 | tf_op jit(solution)/shard_map/ppermute | solution.py:16
  14.9 20.4 %collective-permute-start = (bf16[3,4096]{1,0:T(4,128)(2,1)}, bf16[3,4096]{1,0:T(4,128)(2,1)}, u32[]{:S(2)}, u32[]{:S(2)}) collective-permute-start(bf16[3,4096]{1,0:T(4,128)(2,1)} %slice.153), channel_id=1, source_target_pairs={{0,1},{1,4},{4,5},{5,8},{8,9},{9,12},{12,13},{2,3},{3,6},{6,7},{7,... | collective-permute-start | bytes 73736 | tf_op jit(solution)/shard_map/ppermute | solution.py:16
  26.2 8.0 %copy-start.21 = (f32[64]{0:T(128)}, f32[64]{0:T(128)S(1)}, u32[]{:S(2)}) copy-start(f32[64]{0:T(128)S(1)} %multiply_reduce_fusion.1) | copy-start | bytes 772
  32.2 3.1 copy-start.7
  34.2 2.5 copy-start.15
  34.2 2.5 copy-start.16
  34.2 2.5 copy-start.17
  43.5 13.5 %copy-start.1 = (bf16[256,4096]{0,1:T(8,128)(2,1)}, bf16[256,4096]{0,1:T(8,128)(2,1)S(1)}, u32[]{:S(2)}) copy-start(bf16[256,4096]{0,1:T(8,128)(2,1)S(1)} %copy.78) | copy-start | bytes 6291460
  43.5 5.2 %copy-start.22 = (f32[64]{0:T(128)S(1)}, f32[64]{0:T(128)}, u32[]{:S(2)}) copy-start(f32[64]{0:T(128)} %copy-done.21) | copy-start | bytes 772
  43.5 5.2 %copy-start.30 = (f32[64]{0:T(128)S(1)}, f32[64]{0:T(128)}, u32[]{:S(2)}) copy-start(f32[64]{0:T(128)} %multiply_multiply_fusion.2) | copy-start | bytes 772
  49.3 3.1 copy-start.23
  49.3 5.7 %copy-start.9 = (f32[2,256,64]{1,2,0:T(8,128)S(1)}, f32[2,256,64]{1,2,0:T(8,128)}, u32[]{:S(2)}) copy-start(f32[2,256,64]{1,2,0:T(8,128)} %param.17) | copy-start | bytes 393220
  51.5 302.7 %all-gather.7.cloned.1.call-start = ((), (), s32[]{:S(2)}) async-start(), calls=%async_computation | async-start | bytes 18874368 | tf_op jit(solution)/shard_map/all_gather | solution.py:21
  57.0 6.7 %copy-start.26 = (f32[1,1,64]{2,1,0:T(1,128)S(1)}, f32[1,1,64]{2,1,0:T(1,128)}, u32[]{:S(2)}) copy-start(f32[1,1,64]{2,1,0:T(1,128)} %get-tuple-element.421) | copy-start | bytes 772
  57.0 30.9 %copy-start.20 = (s32[256]{0:T(256)S(1)}, s32[256]{0:T(256)}, u32[]{:S(2)}) copy-start(s32[256]{0:T(256)} %copy-done.19) | copy-start | bytes 3076
  59.2 34.9 %copy-start.10 = (f32[256,64]{1,0:T(8,128)S(1)}, f32[256,64]{1,0:T(8,128)}, u32[]{:S(2)}) copy-start(f32[256,64]{1,0:T(8,128)} %get-tuple-element.418) | copy-start | bytes 196612
  59.2 41.2 %collective-permute-start.2 = (s32[16,2]{0,1:T(2,128)S(1)}, s32[16,2]{0,1:T(2,128)S(1)}, u32[]{:S(2)}, u32[]{:S(2)}) collective-permute-start(s32[16,2]{0,1:T(2,128)S(1)} %copy-done.27), channel_id=1, source_target_pairs={{0,1},{1,4},{4,5},{5,8},{8,9},{9,12},{12,13},{2,3},{3,6},{6,7},{7,... | collective-permute-start | bytes 392 | tf_op jit(solution)/shard_map/ppermute | solution.py:16
  103.3 6.7 %copy-start.12 = (pred[256,256]{1,0:T(8,128)(4,1)S(1)}, pred[256,256]{1,0:T(8,128)(4,1)}, u32[]{:S(2)}) copy-start(pred[256,256]{1,0:T(8,128)(4,1)} %fusion.32) | copy-start | bytes 196612
  103.3 6.7 %copy-start.14 = (f32[64,256]{1,0:T(8,128)S(1)}, f32[64,256]{1,0:T(8,128)}, u32[]{:S(2)}) copy-start(f32[64,256]{1,0:T(8,128)} %get-tuple-element.414) | copy-start | bytes 196612
  110.0 6.3 %copy-start.4 = (bf16[256,64,64]{0,2,1:T(8,128)(2,1)S(1)}, bf16[256,64,64]{0,2,1:T(8,128)(2,1)}, u32[]{:S(2)}) copy-start(bf16[256,64,64]{0,2,1:T(8,128)(2,1)} %rev.22) | copy-start | bytes 6291460
  203.2 31.7 %copy-start.8 = (bf16[256,4,128]{2,0,1:T(8,128)(2,1)S(1)}, bf16[256,4,128]{2,0,1:T(8,128)(2,1)}, u32[]{:S(2)}) copy-start(bf16[256,4,128]{2,0,1:T(8,128)(2,1)} %copy.97) | copy-start | bytes 786436
  372.1 6.1 %copy-start.2 = (bf16[256,4096]{0,1:T(8,128)(2,1)S(1)}, bf16[256,4096]{0,1:T(8,128)(2,1)}, u32[]{:S(2)}) copy-start(bf16[256,4096]{0,1:T(8,128)(2,1)} %copy-done.1) | copy-start | bytes 6291460
  372.1 6.0 %copy-start.13 = (f32[256,64]{0,1:T(8,128)S(1)}, f32[256,64]{0,1:T(8,128)}, u32[]{:S(2)}) copy-start(f32[256,64]{0,1:T(8,128)} %get-tuple-element.422) | copy-start | bytes 196612
  372.1 6.0 %copy-start.29 = (f32[64]{0:T(128)S(1)}, f32[64]{0:T(128)}, u32[]{:S(2)}) copy-start(f32[64]{0:T(128)} %param.21) | copy-start | bytes 772
  396.6 5.8 %copy-start.6 = (bf16[256,4096]{1,0:T(8,128)(2,1)S(1)}, bf16[256,4096]{1,0:T(8,128)(2,1)}, u32[]{:S(2)}) copy-start(bf16[256,4096]{1,0:T(8,128)(2,1)} %param.16) | copy-start | bytes 6291460
  396.6 5.8 %copy-start.18 = (f32[4096]{0:T(1024)S(1)}, f32[4096]{0:T(1024)}, u32[]{:S(2)}) copy-start(f32[4096]{0:T(1024)} %param.22) | copy-start | bytes 49156
  402.4 5.0 %copy-start.24 = (f32[16]{0:T(128)S(1)}, f32[16]{0:T(128)}, u32[]{:S(2)}) copy-start(f32[16]{0:T(128)} %get-tuple-element.437) | copy-start | bytes 196
  402.4 5.0 %copy-start.25 = (s32[16]{0:T(128)S(1)}, s32[16]{0:T(128)}, u32[]{:S(2)}) copy-start(s32[16]{0:T(128)} %get-tuple-element.438) | copy-start | bytes 196
  402.4 7.6 %copy-start.28 = (s32[16,2]{0,1:T(2,128)S(1)}, s32[16,2]{0,1:T(2,128)}, u32[]{:S(2)}) copy-start(s32[16,2]{0,1:T(2,128)} %param.23) | copy-start | bytes 388
  407.4 9.2 %copy-start.5 = (bf16[256,4096]{1,0:T(8,128)(2,1)}, bf16[256,4096]{1,0:T(8,128)(2,1)S(1)}, u32[]{:S(2)}) copy-start(bf16[256,4096]{1,0:T(8,128)(2,1)S(1)} %multiply_convert_fusion) | copy-start | bytes 6291460
  407.8 7.7 %collective-permute-start.3 = (f32[16,4096]{1,0:T(8,128)S(1)}, f32[16,4096]{1,0:T(8,128)S(1)}, u32[]{:S(2)}, u32[]{:S(2)}) collective-permute-start(f32[16,4096]{1,0:T(8,128)S(1)} %convolution_divide_fusion), channel_id=1, source_target_pairs={{1,0},{4,1},{5,4},{8,5},{9,8},{12,9},{13,12},{3,2},{6,3},{7,6},{10... | collective-permute-start | bytes 786440 | tf_op jit(solution)/shard_map/ppermute | solution.py:16
  (5 other events, 8.3 us)
Sparse Core Ops, SparseCore 0:
  51.6 151.5 all-gather.8
  204.8 149.2 all-gather.6
where the time goes:
time: 425 us; the launch traced here: 423 us
  waiting for transfers between devices  191 us (45%)
  other arithmetic  86.9 us (20%)
  local copies, waits for them, and re-layouts  55.8 us (13%)
  matrix products  36.5 us (9%)
  blocking collectives  24.2 us (6%)
  between operations  16.6 us (4%)
  starting transfers between devices  12.4 us (3%)
    all_gather x2, waiting for transfers between devices, carried_in(): everything = jax.tree.map(lambda part: lax.all_gather(part, axis), x)  185 us
    select_n x16, other arithmetic, lap(): return jax.tree.map(lambda a, b: jnp.where(reached, a, b), new, before)  48.2 us
    all_gather x2, blocking collectives, carried_in(): everything = jax.tree.map(lambda part: lax.all_gather(part, axis), x)  24.2 us
    dot_general x2, matrix products, stretch_parts(): jnp.einsum('hij,jhp->ihp', mixing, x_block, preferred_element_type=jnp.fl...  16.4 us
    dot_general x2, matrix products, finish(): jnp.einsum('cihn,chpn->cihp', c_heads, seeded, precision=lax.Precision.HI...  13.6 us
    convert_element_type x2, other arithmetic, stretch_parts(): mixing = (scores * decays * scale_block.T[:, None, :]).astype(jnp.bfloat16)  12.6 us
    ppermute x4, starting transfers between devices, from_behind(): return lax.ppermute(block, axis, route)  12.3 us
    unnamed x70, local copies, waits for them, and re-layouts  9.7 us
  transfers between devices with their start and end apart: 6, of which 3 were waited for; matrix products, arithmetic and copies ran while one was open for 25% of the time, Pallas kernels for 0%

commit v1 on v0

v1 whole, which is shorter than its diff:
```python
import functools
import jax
import jax.numpy as jnp
from jax import lax
from jax.experimental import pallas as pl
from jax.experimental.pallas import tpu as pltpu
from jax.sharding import PartitionSpec as P

HEADDIM = 64
STATE = 128
GROUPS = 8
PER = 16
LOG2E = 1.4426950408889634
BIG = 160.0
HALO = 8
MESH = pl.DeviceIdType.MESH


def silu(v):
    return v / (1.0 + jnp.exp(-v))


def conv(rim, block, taps):
    padded = jnp.concatenate([rim.astype(jnp.float32), block.astype(jnp.float32)], axis=0)
    total = taps[3:4] * padded[HALO:]
    for k in range(3):
        total = total + taps[k : k + 1] * pltpu.roll(padded, 3 - k, 0)[HALO:]
    return silu(total).astype(jnp.bfloat16)


def dot(a, b):
    return jnp.dot(a, b, preferred_element_type=jnp.float32)


def kernel(
    chips,
    groups,
    x_ref, bc_ref, gate_ref, rate_ref, lw_ref, taps_x, taps_bc, skip_ref, gain_ref, span_ref,
    out_ref, pool_ref,
    halo_x, halo_bc, span_in, xc, bs, cs, colt, rowt, lead_hl, expand, y_acc, h_lead,
    s_own, t_own, s_send, t_send, s_in, t_in, chain_in, follow_in, chain_out,
    own_pool, spill_out, spill_in,
    sem_halo, sem_s, sem_t, sem_chain, sem_follow, sem_spill,
):
    tokens = x_ref.shape[0]
    width = PER * HEADDIM
    half = tokens // 2
    c = lax.axis_index("ctx")
    d = lax.axis_index("dp")
    other = 1 - d
    nxt = c + 2 * d - 1
    prv = c - 2 * d + 1
    pos = d * c + (1 - d) * (chips - 1 - c)
    has_next = pos < chips - 1
    has_prev = pos > 0
    index = c * 2 + d
    last_index = chips * 2 - 1
    partner = {"ctx": c, "dp": other}
    halo_to = {"ctx": d * nxt + (1 - d) * c, "dp": other}
    spill_to = {"ctx": d * c + (1 - d) * nxt, "dp": other}
    follow_chain = {"ctx": nxt, "dp": d}

    barrier = pltpu.get_barrier_semaphore()
    pl.semaphore_signal(barrier, inc=1, device_id=partner, device_id_type=MESH)

    @pl.when(has_next)
    def _():
        pl.semaphore_signal(barrier, inc=1, device_id={"ctx": nxt, "dp": other}, device_id_type=MESH)
        pl.semaphore_signal(barrier, inc=1, device_id={"ctx": nxt, "dp": d}, device_id_type=MESH)

    @pl.when(has_prev)
    def _():
        pl.semaphore_signal(barrier, inc=1, device_id={"ctx": prv, "dp": d}, device_id_type=MESH)

    pl.semaphore_wait(barrier, 1 + 2 * has_next.astype(jnp.int32) + has_prev.astype(jnp.int32))

    def remote(src, dst, sems, k, to):
        return pltpu.make_async_remote_copy(
            src_ref=src, dst_ref=dst, send_sem=sems.at[0, k], recv_sem=sems.at[1, k],
            device_id=to, device_id_type=MESH,
        )

    tail = pl.ds(tokens - HALO, HALO)
    halos = (
        remote(x_ref.at[tail], halo_x, sem_halo, 0, halo_to),
        remote(bc_ref.at[tail], halo_bc, sem_halo, 1, halo_to),
        remote(span_ref, span_in, sem_halo, 2, halo_to),
    )

    @pl.when(index < last_index)
    def _():
        for copy in halos:
            copy.start()

    def s_copy(g):
        return remote(s_send.at[g], s_in.at[g], sem_s, g, partner)

    def t_copy(g):
        return remote(t_send.at[g], t_in.at[g], sem_t, g, partner)

    def chain_copy(g):
        return remote(chain_out.at[g], chain_in.at[g], sem_chain, g, follow_chain)

    def follow_copy(g):
        return remote(chain_in.at[g], follow_in.at[g], sem_follow, g, partner)

    def spill_copy(g):
        return remote(spill_out.at[g], spill_in.at[g], sem_spill, g, spill_to)

    rows = lax.broadcasted_iota(jnp.int32, (tokens, tokens), 0)
    cols = lax.broadcasted_iota(jnp.int32, (tokens, tokens), 1)
    tri = (rows >= cols).astype(jnp.float32)
    lane = lax.broadcasted_iota(jnp.int32, (tokens, 128), 1)
    is_fwd = lane < PER
    live = lane < 2 * PER
    erow = lax.rem(lax.broadcasted_iota(jnp.int32, (128, width), 0), 2 * PER)
    ebelow = lax.broadcasted_iota(jnp.int32, (128, width), 0) < 4 * PER
    ehead = lax.div(lax.broadcasted_iota(jnp.int32, (128, width), 1), HEADDIM)
    expand[0] = ((erow == ehead + PER * (1 - d)) & ebelow).astype(jnp.float32).astype(jnp.bfloat16)
    expand[1] = ((erow == ehead + PER * d) & ebelow).astype(jnp.float32).astype(jnp.bfloat16)

    @pl.when(index == 0)
    def _():
        halo_x[...] = jnp.zeros_like(halo_x)
        halo_bc[...] = jnp.zeros_like(halo_bc)
        span_in[...] = jnp.zeros_like(span_in)

    @pl.when(index > 0)
    def _():
        for copy in halos:
            copy.wait_recv()

    def hi_lo(v):
        v = jnp.where(live[: v.shape[0]], v, 0.0)
        hi = v.astype(jnp.bfloat16).astype(jnp.float32)
        return (hi + pltpu.roll(v - hi, 2 * PER, 1)).astype(jnp.bfloat16)

    @pl.loop(0, groups)
    def _(g):
        wide = pl.ds(pl.multiple_of(g * width, width), width)
        b_at = pl.ds(pl.multiple_of(g * STATE, STATE), STATE)
        c_at = pl.ds(pl.multiple_of((groups + g) * STATE, STATE), STATE)
        b_g = conv(halo_bc[:, b_at], bc_ref[:, b_at], taps_bc[:, b_at])
        bs[g] = b_g
        cs[g] = conv(halo_bc[:, c_at], bc_ref[:, c_at], taps_bc[:, c_at])
        cum = lax.dot(tri, rate_ref[g], precision=lax.Precision.HIGHEST,
                      preferred_element_type=jnp.float32)
        col = jnp.where(is_fwd, cum, -cum)
        row = lw_ref[g] - col
        colt[g] = col
        rowt[g] = row.T
        end = cum[tokens - 1 : tokens]
        to_end = hi_lo(jnp.exp2(row + jnp.where(is_fwd, end, 0.0)))
        lead_hl[g] = hi_lo(jnp.exp2(jnp.where(is_fwd, cum, end - cum)))
        total = hi_lo(jnp.broadcast_to(jnp.exp2(end), (16, 128)))
        x_g = conv(halo_x[:, wide], x_ref[:, wide], taps_x[:, wide])
        xc[g] = x_g
        xf = x_g.astype(jnp.float32)
        across = (((0,), (0,)), ((), ()))
        sent = (xf * dot(to_end, expand[1])).astype(jnp.bfloat16)
        s_send[g] = lax.dot_general(b_g, sent, across, preferred_element_type=jnp.float32).astype(jnp.bfloat16)
        t_send[g] = dot(total, expand[1])[:8]
        s_copy(g).start()
        t_copy(g).start()
        kept = (xf * dot(to_end, expand[0])).astype(jnp.bfloat16)
        s_own[g] = lax.dot_general(b_g, kept, across, preferred_element_type=jnp.float32)
        t_own[g] = dot(total, expand[0])[:8]

    def relay(g):
        s_copy(g).wait_recv()
        t_copy(g).wait_recv()

        @pl.when(has_prev)
        def _():
            chain_copy(g).wait_recv()

        @pl.when(pos == 0)
        def _():
            chain_in[g] = jnp.zeros_like(chain_in[g])

        follow_copy(g).start()
        state = t_in[g][0:1] * chain_in[g].astype(jnp.float32) + s_in[g].astype(jnp.float32)
        h_lead[g] = state.astype(jnp.bfloat16)

        @pl.when(has_next)
        def _():
            chain_out[g] = (t_own[g][0:1] * state + s_own[g]).astype(jnp.bfloat16)
            chain_copy(g).start()

    slots = 2 * groups

    left = lax.broadcasted_iota(jnp.int32, (tokens, 128), 1) < HEADDIM
    lower = rows[:half, :half] >= cols[:half, :half]

    @pl.loop(0, groups)
    def _(g):
        score = lax.dot_general(cs[g], bs[g], (((1,), (1,)), ((), ())), preferred_element_type=jnp.float32)
        for part in range(2):
            turn = 2 * g + part - 2 * pos

            @pl.when((turn >= 0) & (turn < groups))
            def _():
                relay(turn)

            for pair in range(part * PER // 4, (part + 1) * PER // 4):
                at = pair * 2 * HEADDIM
                x_pair = xc[g, :, at : at + 2 * HEADDIM]
                got = []
                for head in (2 * pair, 2 * pair + 1):
                    cf = colt[g, :, head : head + 1]
                    cb = colt[g, :, PER + head : PER + head + 1]
                    rf = rowt[g, head : head + 1, :]
                    rb = rowt[g, PER + head : PER + head + 1, :]
                    tl = jnp.where(lower, cf[:half] + rf[:, :half], cb[:half] + rb[:, :half])
                    tr = cb[:half] + rb[:, half:]
                    bl = cf[half:] + rf[:, :half]
                    br = jnp.where(lower, cf[half:] + rf[:, half:], cb[half:] + rb[:, half:])
                    top = jnp.concatenate([tl, tr], axis=1)
                    bottom = jnp.concatenate([bl, br], axis=1)
                    mix_top = (score[:half] * jnp.exp2(top)).astype(jnp.bfloat16)
                    mix_bottom = (score[half:] * jnp.exp2(bottom)).astype(jnp.bfloat16)
                    got.append(dot(jnp.concatenate([mix_top, mix_bottom], axis=0), x_pair))
                y_acc[g, :, at : at + 2 * HEADDIM] = jnp.where(left, got[0], got[1])

    vis = span_ref.shape[0]
    spans = jnp.concatenate([span_ref[...], span_in[...]], axis=0)
    token = index * tokens + lax.broadcasted_iota(jnp.int32, (2 * vis, tokens), 1)
    inside = ((token >= spans[:, 0:1]) & (token < spans[:, 1:2])).astype(jnp.float32).astype(jnp.bfloat16)
    length = jnp.maximum(spans[:vis, 1:2] - spans[:vis, 0:1], 1).astype(jnp.float32)

    @pl.loop(0, groups)
    def _(g):
        @pl.when(g + 2 * pos >= slots)
        def _():
            relay(g)

        wide = pl.ds(pl.multiple_of(g * width, width), width)
        c_g = cs[g]
        lead = dot(lead_hl[g], expand[0]) * dot(c_g, h_lead[g])
        mixed = y_acc[g] + lead + skip_ref[:, wide] * xc[g].astype(jnp.float32)
        follow_copy(g).wait_recv()
        mixed = mixed + dot(lead_hl[g], expand[1]) * dot(c_g, follow_in[g])
        gated = mixed * silu(gate_ref[:, wide].astype(jnp.float32))
        mean_sq = jnp.mean(gated * gated, axis=1, keepdims=True)
        token_out = (gated * lax.rsqrt(mean_sq + 1e-05) * gain_ref[:, wide]).astype(jnp.bfloat16)
        out_ref[:, wide] = token_out
        sums = dot(inside, token_out)
        own_pool[g] = sums[:vis]
        spill_out[g] = sums[vis:]

        @pl.when(index > 0)
        def _():
            spill_copy(g).start()

    @pl.loop(0, groups)
    def _(g):
        wide = pl.ds(pl.multiple_of(g * width, width), width)

        @pl.when(index < last_index)
        def _():
            spill_copy(g).wait_recv()
            pool_ref[:, wide] = ((own_pool[g] + spill_in[g]) / length).astype(jnp.bfloat16)

        @pl.when(index == last_index)
        def _():
            pool_ref[:, wide] = (own_pool[g] / length).astype(jnp.bfloat16)

    @pl.loop(0, groups)
    def _(g):
        s_copy(g).wait_send()
        t_copy(g).wait_send()
        follow_copy(g).wait_send()

        @pl.when(has_next)
        def _():
            chain_copy(g).wait_send()

        @pl.when(index > 0)
        def _():
            spill_copy(g).wait_send()

    @pl.when(index < last_index)
    def _():
        for copy in halos:
            copy.wait_send()


def on_device(
    x_in, bc_in, gate_z, log_decay, resets, conv_x, conv_bc, skip_d, norm_gain, visit_span
):
    tokens, channels = x_in.shape
    groups = bc_in.shape[2] // STATE
    width = PER * HEADDIM
    vis = visit_span.shape[0]

    def by_group(v):
        v = v.reshape(2, tokens, groups, PER).transpose(2, 1, 0, 3).reshape(groups, tokens, 2 * PER)
        return jnp.pad(v, ((0, 0), (0, 0), (0, 128 - 2 * PER)))

    rate = by_group(log_decay * LOG2E - BIG * resets.astype(jnp.float32)[None, :, None])
    log_weight = by_group(jnp.maximum(0.5 * jnp.log2(-jnp.expm1(2.0 * log_decay)), -1000.0))
    spans = jnp.pad(visit_span, ((0, 0), (0, 126)))
    f32, bf16 = jnp.float32, jnp.bfloat16
    state = (groups, STATE, width)
    whole = pl.BlockSpec(memory_space=pltpu.VMEM)
    pair = pltpu.SemaphoreType.DMA((2, groups))
    return pl.pallas_call(
        functools.partial(kernel, lax.axis_size("ctx"), groups),
        out_shape=(
            jax.ShapeDtypeStruct((tokens, channels), bf16),
            jax.ShapeDtypeStruct((vis, channels), bf16),
        ),
        in_specs=[whole] * 10,
        out_specs=(whole, whole),
        scratch_shapes=[
            pltpu.VMEM((HALO, channels), bf16),
            pltpu.VMEM((HALO, 2 * groups * STATE), bf16),
            pltpu.VMEM((vis, 128), jnp.int32),
            pltpu.VMEM((groups, tokens, width), bf16),
            pltpu.VMEM((groups, tokens, STATE), bf16),
            pltpu.VMEM((groups, tokens, STATE), bf16),
            pltpu.VMEM((groups, tokens, 128), f32),
            pltpu.VMEM((groups, 128, tokens), f32),
            pltpu.VMEM((groups, tokens, 128), bf16),
            pltpu.VMEM((2, 128, width), bf16),
            pltpu.VMEM((groups, tokens, width), f32),
            pltpu.VMEM(state, bf16),
            pltpu.VMEM(state, f32),
            pltpu.VMEM((groups, 8, width), f32),
            pltpu.VMEM(state, bf16),
            pltpu.VMEM((groups, 8, width), f32),
            pltpu.VMEM(state, bf16),
            pltpu.VMEM((groups, 8, width), f32),
            pltpu.VMEM(state, bf16),
            pltpu.VMEM(state, bf16),
            pltpu.VMEM(state, bf16),
            pltpu.VMEM((groups, vis, width), f32),
            pltpu.VMEM((groups, vis, width), f32),
            pltpu.VMEM((groups, vis, width), f32),
            pltpu.SemaphoreType.DMA((2, 3)),
            pair, pair, pair, pair, pair,
        ],
        compiler_params=pltpu.CompilerParams(
            collective_id=0, has_side_effects=True, vmem_limit_bytes=60 << 20
        ),
    )(
        x_in,
        bc_in.reshape(tokens, 2 * groups * STATE),
        gate_z,
        rate,
        log_weight,
        conv_x,
        conv_bc.reshape(4, 2 * groups * STATE),
        jnp.repeat(skip_d, HEADDIM)[None, :],
        norm_gain[None, :],
        spans,
    )


def solution(mesh):
    return jax.shard_map(
        on_device,
        mesh=mesh,
        in_specs=(
            P(("groups", "ctx", "dp"), "tp"),
            P(("groups", "ctx", "dp"), None, "tp"),
            P(("groups", "ctx", "dp"), "tp"),
            P(None, ("groups", "ctx", "dp"), "tp"),
            P(("groups", "ctx", "dp")),
            P(None, "tp"),
            P(None, None, "tp"),
            P("tp"),
            P("tp"),
            P(("groups", "ctx", "dp"), None),
        ),
        out_specs=(P(("groups", "ctx", "dp"), "tp"), P(("groups", "ctx", "dp"), "tp")),
        check_vma=False,
    )
```

time: 425 us -> 64 us (0.15)
  waiting for transfers between devices: 191 us -> 0 us
  other arithmetic: 86.9 us -> 1.73 us
  Pallas kernels: 0 us -> 50.4 us
  local copies, waits for them, and re-layouts: 55.8 us -> 10.9 us
  matrix products: 36.5 us -> 0 us
  blocking collectives: 24.2 us -> 0 us
  between operations: 16.6 us -> 0.69 us
  starting transfers between devices: 12.4 us -> 0 us
    all_gather x2 -> x0, waiting for transfers between devices: 185 us -> none  [carried_in(): everything = jax.tree.map(lambda part: lax.all_gather(part, axis), x)]
    pallas_call x0 -> x1, Pallas kernels: none -> 50.4 us  [on_device(): pl.pallas_call(functools.partial(kernel, lax.axis_size('ctx'), groups), o...]
    select_n x16 -> x0, other arithmetic: 48.2 us -> none  [lap(): return jax.tree.map(lambda a, b: jnp.where(reached, a, b), new, before)]
    dot_general x10 -> x0, matrix products: 36.5 us -> none  [the longest x2 16.4 us: stretch_parts(): jnp.einsum('hij,jhp->ihp', mixing, x_block, preferred_element_type=jnp.fl...]
    convert_element_type x11 -> x0, other arithmetic: 25.8 us -> none  [the longest x2 12.6 us: stretch_parts(): mixing = (scores * decays * scale_block.T[:, None, :]).astype(jnp.bfloat16)]
    all_gather x2 -> x0, blocking collectives: 24.2 us -> none  [carried_in(): everything = jax.tree.map(lambda part: lax.all_gather(part, axis), x)]
    rev x7 -> x0, local copies, waits for them, and re-layouts: 14.2 us -> none  [the longest x1 7.28 us: on_device(): bwd_y = jnp.flip(finish(bwd_parts, c_rev, bwd_in), 0)]
    ppermute x4 -> x0, starting transfers between devices: 12.3 us -> none  [from_behind(): return lax.ppermute(block, axis, route)]
  transfers between devices with their start and end apart: 6 -> 0, of which waited for: 3 -> 0; matrix products, arithmetic and copies ran while one was open for 25% -> 0% of each run, Pallas kernels for 0% -> 0%
where the time goes in v1:
time: 64 us; the launch traced here: 63.7 us
  Pallas kernels  50.4 us (79%)
  local copies, waits for them, and re-layouts  10.9 us (17%)
  other arithmetic  1.73 us (3%)
  between operations  0.69 us (1%)
    pallas_call x1, Pallas kernels, on_device(): pl.pallas_call(functools.partial(kernel, lax.axis_size('ctx'), groups), o...  50.4 us
    unnamed x9, local copies, waits for them, and re-layouts  6.78 us
    pad x2, local copies, waits for them, and re-layouts, by_group(): return jnp.pad(v, ((0, 0), (0, 0), (0, 128 - 2 * PER)))  1.69 us

profile of v1, /device:TPU:1, one launch (start us, length us, event | category | flops | bytes accessed | tf_op | source)
XLA Modules:
  0.0 63.7 jit_solution(7146255118912382062)
XLA Ops:
  0.6 0.7 %convert_multiply_fusion = f32[256]{0:T(256)S(1)} fusion(s32[256]{0:T(256)} %param.14), kind=kLoop, calls=%fused_computation.2 | loop fusion | flops 512 | bytes 2048 | tf_op jit(solution)/shard_map/mul | solution.py:300
  1.3 0.8 %copy.22 = s32[16,2]{1,0:T(8,128)S(1)} copy(s32[16,2]{0,1:T(2,128)} %param.19) | data formatting | bytes 256 | tf_op args[9]
  2.1 0.6 pad.13.span_ref
  2.7 1.3 %copy.24 = f32[1,4,2,512]{3,1,2,0:T(4,128)} copy(f32[1,4,2,512]{3,2,1,0:T(2,128)} %bitcast.21) | data formatting | bytes 32768
  4.0 0.7 %broadcast_in_dim.7 = f32[64,64]{1,0:T(8,128)S(1)} broadcast(f32[64]{0:T(128)} %param.17), dimensions={0} | broadcast | bytes 16640 | tf_op jit(solution)/shard_map/broadcast_in_dim | solution.py:354
  4.7 0.7 %broadcast_in_dim_reshape.3.skip_ref = f32[1,4096]{1,0:T(1,128)} reshape(f32[64,64]{1,0:T(8,128)S(1)} %broadcast_in_dim.7) | data formatting | bytes 32768 | tf_op jit(solution)/shard_map/broadcast_in_dim;reshape | solution.py:354
  5.4 0.0 copy-start
  5.4 1.0 %multiply_maximum_fusion = (f32[2,256,64]{1,2,0:T(8,128)S(1)}, f32[2,256,64]{1,2,0:T(8,128)S(1)}) fusion(f32[2,256,64]{1,2,0:T(8,128)} %param.13, f32[256]{0:T(256)S(1)} %convert_multiply_fusion), kind=kLoop, calls=%fused_computation | loop fusion | flops 196608 | bytes 394240 | tf_op jit(solution)/shard_map/max | solution.py:301
  6.5 0.2 copy.19
  6.7 0.8 %pad.11.rate_ref = f32[4,256,128]{2,1,0:T(8,128)} pad(f32[4,256,32]{2,1,0:T(8,128)S(1)} %copy.19, f32[]{:T(128)} %constant.4.clone.1), padding=0_0x0_0x0_96 | pad | bytes 655364 | tf_op jit(solution)/shard_map/jit(_pad)/pad | solution.py:298
  7.5 0.2 copy.21
  7.7 0.9 %pad.12.lw_ref = f32[4,256,128]{2,1,0:T(8,128)} pad(f32[4,256,32]{2,1,0:T(8,128)S(1)} %copy.21, f32[]{:T(128)} %constant.4.clone.1), padding=0_0x0_0x0_96 | pad | bytes 655364 | tf_op jit(solution)/shard_map/jit(_pad)/pad | solution.py:298
  8.6 0.0 copy-done
  8.6 0.9 %copy.23 = bf16[32,8,2,512]{3,1,2,0:T(8,128)(2,1)} copy(bf16[32,8,2,512]{3,2,1,0:T(2,128)(2,1)S(1)} %bitcast.18) | data formatting | bytes 1048576
  9.5 50.4 %shard_map.113 = (bf16[256,4096]{1,0:T(8,128)(2,1)}, bf16[16,4096]{1,0:T(8,128)(2,1)}) custom-call(bf16[256,4096]{1,0:T(8,128)(2,1)} %x_ref.1, bf16[256,1024]{1,0:T(8,128)(2,1)} %bitcast.13, bf16[256,4096]{1,0:T(8,128)(2,1)} %gate_ref.1, f32[4,256,128]{2,1,0:T(8,128)} %pad.11.rate_ref, f32[4,256,128]{2,1,0:T(8,128)} %pad.12.lw_ref, f32[4,4096]{1,0:T(4,128)} %taps_x.1, ...), custom_call_target="tpu_custom_call" | custom-call | tf_op jit(solution)/shard_map/pallas_call | solution.py:307
  59.8 0.0 copy-start.1
  59.9 3.2 %copy.27 = bf16[256,4096]{1,0:T(8,128)(2,1)} copy(bf16[256,4096]{1,0:T(8,128)(2,1)} %get-tuple-element.6) | data formatting | bytes 4194304
  63.0 0.0 copy-done.1
  63.0 0.7 %copy.28 = bf16[16,4096]{1,0:T(8,128)(2,1)} copy(bf16[16,4096]{1,0:T(8,128)(2,1)S(1)} %copy-done.1) | data formatting | bytes 262144
  (2 shorter events, 0.0 us)
Async XLA Ops:
  5.4 3.2 %copy-start = (bf16[256,2,512]{2,1,0:T(2,128)(2,1)S(1)}, bf16[256,2,512]{2,1,0:T(2,128)(2,1)}, u32[]{:S(2)}) copy-start(bf16[256,2,512]{2,1,0:T(2,128)(2,1)} %param.11) | copy-start | bytes 1572868
  59.8 3.2 %copy-start.1 = (bf16[16,4096]{1,0:T(8,128)(2,1)S(1)}, bf16[16,4096]{1,0:T(8,128)(2,1)}, u32[]{:S(2)}) copy-start(bf16[16,4096]{1,0:T(8,128)(2,1)} %get-tuple-element.7) | copy-start | bytes 393220

commit v2 on v1

--- a/solution.py
+++ b/solution.py
@@ -12,6 +12,7 @@
 PER = 16
 LOG2E = 1.4426950408889634
 BIG = 160.0
+LIMIT = 34
 HALO = 8
 MESH = pl.DeviceIdType.MESH
 
@@ -22,9 +23,9 @@
 
 def conv(rim, block, taps):
     padded = jnp.concatenate([rim.astype(jnp.float32), block.astype(jnp.float32)], axis=0)
-    total = taps[3:4] * padded[HALO:]
+    total = taps[3] * padded[HALO:]
     for k in range(3):
-        total = total + taps[k : k + 1] * pltpu.roll(padded, 3 - k, 0)[HALO:]
+        total = total + taps[k] * pltpu.roll(padded, 3 - k, 0)[HALO:]
     return silu(total).astype(jnp.bfloat16)
 
 
@@ -35,7 +36,7 @@
 def kernel(
     chips,
     groups,
-    x_ref, bc_ref, gate_ref, rate_ref, lw_ref, taps_x, taps_bc, skip_ref, gain_ref, span_ref,
+    x_ref, bc_ref, gate_ref, rate_ref, reset_ref, taps_x, taps_bc, skip_ref, gain_ref, span_ref,
     out_ref, pool_ref,
     halo_x, halo_bc, span_in, xc, bs, cs, colt, rowt, lead_hl, expand, y_acc, h_lead,
     s_own, t_own, s_send, t_send, s_in, t_in, chain_in, follow_in, chain_out,
@@ -110,14 +111,12 @@
     rows = lax.broadcasted_iota(jnp.int32, (tokens, tokens), 0)
     cols = lax.broadcasted_iota(jnp.int32, (tokens, tokens), 1)
     tri = (rows >= cols).astype(jnp.float32)
-    lane = lax.broadcasted_iota(jnp.int32, (tokens, 128), 1)
-    is_fwd = lane < PER
-    live = lane < 2 * PER
-    erow = lax.rem(lax.broadcasted_iota(jnp.int32, (128, width), 0), 2 * PER)
-    ebelow = lax.broadcasted_iota(jnp.int32, (128, width), 0) < 4 * PER
-    ehead = lax.div(lax.broadcasted_iota(jnp.int32, (128, width), 1), HEADDIM)
-    expand[0] = ((erow == ehead + PER * (1 - d)) & ebelow).astype(jnp.float32).astype(jnp.bfloat16)
-    expand[1] = ((erow == ehead + PER * d) & ebelow).astype(jnp.float32).astype(jnp.bfloat16)
+    is_fwd = lax.broadcasted_iota(jnp.int32, (2 * PER, tokens), 0) < PER
+    erow = lax.rem(lax.broadcasted_iota(jnp.int32, (4 * PER, width), 0), 2 * PER)
+    ehead = lax.div(lax.broadcasted_iota(jnp.int32, (4 * PER, width), 1), HEADDIM)
+    expand[0] = (erow == ehead + PER * (1 - d)).astype(jnp.float32).astype(jnp.bfloat16)
+    expand[1] = (erow == ehead + PER * d).astype(jnp.float32).astype(jnp.bfloat16)
+    fold = BIG * reset_ref[...].astype(jnp.float32)
 
     @pl.when(index == 0)
     def _():
@@ -130,41 +129,58 @@
         for copy in halos:
             copy.wait_recv()
 
+    across = (((0,), (0,)), ((), ()))
+
     def hi_lo(v):
-        v = jnp.where(live[: v.shape[0]], v, 0.0)
-        hi = v.astype(jnp.bfloat16).astype(jnp.float32)
-        return (hi + pltpu.roll(v - hi, 2 * PER, 1)).astype(jnp.bfloat16)
+        hi = v.astype(jnp.bfloat16)
+        lo = (v - hi.astype(jnp.float32)).astype(jnp.bfloat16)
+        return jnp.concatenate([hi, lo], axis=0)
+
+    def spread(v, which):
+        return lax.dot_general(v, expand[which], across, preferred_element_type=jnp.float32)
+
+    def spread_end(v, which):
+        picked = expand[which, : 2 * PER].astype(jnp.float32) * v
+        return jnp.broadcast_to(jnp.sum(picked, axis=0, keepdims=True), (8, width))
+
+    def taps_of(ref, which, at):
+        return [ref[k, which : which + 1, at] for k in range(4)]
 
     @pl.loop(0, groups)
     def _(g):
         wide = pl.ds(pl.multiple_of(g * width, width), width)
         b_at = pl.ds(pl.multiple_of(g * STATE, STATE), STATE)
         c_at = pl.ds(pl.multiple_of((groups + g) * STATE, STATE), STATE)
-        b_g = conv(halo_bc[:, b_at], bc_ref[:, b_at], taps_bc[:, b_at])
+        b_g = conv(halo_bc[:, b_at], bc_ref[:, b_at], taps_of(taps_bc, 0, b_at))
         bs[g] = b_g
-        cs[g] = conv(halo_bc[:, c_at], bc_ref[:, c_at], taps_bc[:, c_at])
-        cum = lax.dot(tri, rate_ref[g], precision=lax.Precision.HIGHEST,
-                      preferred_element_type=jnp.float32)
+        cs[g] = conv(halo_bc[:, c_at], bc_ref[:, c_at], taps_of(taps_bc, 1, b_at))
+        heads = pl.ds(pl.multiple_of(g * PER, PER), PER)
+        rate = jnp.concatenate([rate_ref[0, heads, :], rate_ref[1, heads, :]], axis=0)
+        cum = lax.dot_general(rate * LOG2E - fold, tri, (((1,), (1,)), ((), ())),
+                              precision=lax.Precision.HIGHEST, preferred_element_type=jnp.float32)
+        r = -2.0 * rate
+        small = r * (1.0 - r * (1 / 2 - r * (1 / 6 - r * (1 / 24 - r * (1 / 120 - r / 720)))))
+        loss = jnp.where(r < 0.25, small, 1.0 - jnp.exp(-r))
+        log_weight = jnp.maximum((0.5 * LOG2E) * jnp.log(loss), -1000.0)
         col = jnp.where(is_fwd, cum, -cum)
-        row = lw_ref[g] - col
-        colt[g] = col
-        rowt[g] = row.T
-        end = cum[tokens - 1 : tokens]
+        row = log_weight - col
+        colt[g] = col.T
+        rowt[g] = row
+        end = cum[:, tokens - 1 : tokens]
         to_end = hi_lo(jnp.exp2(row + jnp.where(is_fwd, end, 0.0)))
         lead_hl[g] = hi_lo(jnp.exp2(jnp.where(is_fwd, cum, end - cum)))
-        total = hi_lo(jnp.broadcast_to(jnp.exp2(end), (16, 128)))
-        x_g = conv(halo_x[:, wide], x_ref[:, wide], taps_x[:, wide])
+        total = jnp.exp2(end)
+        x_g = conv(halo_x[:, wide], x_ref[:, wide], [taps_x[k : k + 1, wide] for k in range(4)])
         xc[g] = x_g
         xf = x_g.astype(jnp.float32)
-        across = (((0,), (0,)), ((), ()))
-        sent = (xf * dot(to_end, expand[1])).astype(jnp.bfloat16)
+        sent = (xf * spread(to_end, 1)).astype(jnp.bfloat16)
         s_send[g] = lax.dot_general(b_g, sent, across, preferred_element_type=jnp.float32).astype(jnp.bfloat16)
-        t_send[g] = dot(total, expand[1])[:8]
+        t_send[g] = spread_end(total, 1)
         s_copy(g).start()
         t_copy(g).start()
-        kept = (xf * dot(to_end, expand[0])).astype(jnp.bfloat16)
+        kept = (xf * spread(to_end, 0)).astype(jnp.bfloat16)
         s_own[g] = lax.dot_general(b_g, kept, across, preferred_element_type=jnp.float32)
-        t_own[g] = dot(total, expand[0])[:8]
+        t_own[g] = spread_end(total, 0)
 
     def relay(g):
         s_copy(g).wait_recv()
@@ -222,11 +238,24 @@
                     got.append(dot(jnp.concatenate([mix_top, mix_bottom], axis=0), x_pair))
                 y_acc[g, :, at : at + 2 * HEADDIM] = jnp.where(left, got[0], got[1])
 
-    vis = span_ref.shape[0]
-    spans = jnp.concatenate([span_ref[...], span_in[...]], axis=0)
-    token = index * tokens + lax.broadcasted_iota(jnp.int32, (2 * vis, tokens), 1)
-    inside = ((token >= spans[:, 0:1]) & (token < spans[:, 1:2])).astype(jnp.float32).astype(jnp.bfloat16)
-    length = jnp.maximum(spans[:vis, 1:2] - spans[:vis, 0:1], 1).astype(jnp.float32)
+    vis = span_ref.shape[1]
+    token = index * tokens + lax.broadcasted_iota(jnp.int32, (tokens, vis), 0)
+
+    def covers(ref):
+        return ((token >= ref[0:1]) & (token < ref[1:2])).astype(jnp.float32).T
+
+    inside = jnp.concatenate([covers(span_ref), covers(span_in)], axis=0).astype(jnp.bfloat16)
+    same = lax.broadcasted_iota(jnp.int32, (vis, vis), 0) == lax.broadcasted_iota(jnp.int32, (vis, vis), 1)
+    spanned = jnp.maximum(span_ref[1:2] - span_ref[0:1], 1).astype(jnp.float32)
+    length = jnp.sum(jnp.where(same, spanned, 0.0), axis=1, keepdims=True)
+
+    def skip_of(g):
+        at = lax.broadcasted_iota(jnp.int32, (groups * PER, width), 0)
+        head = lax.div(lax.broadcasted_iota(jnp.int32, (groups * PER, width), 1), HEADDIM)
+        pick = (at == head + g * PER).astype(jnp.float32)
+        skips = jnp.broadcast_to(skip_ref[...], (8, groups * PER))
+        return lax.dot(skips, pick, precision=lax.Precision.HIGHEST,
+                       preferred_element_type=jnp.float32)[0:1]
 
     @pl.loop(0, groups)
     def _(g):
@@ -236,10 +265,10 @@
 
         wide = pl.ds(pl.multiple_of(g * width, width), width)
         c_g = cs[g]
-        lead = dot(lead_hl[g], expand[0]) * dot(c_g, h_lead[g])
-        mixed = y_acc[g] + lead + skip_ref[:, wide] * xc[g].astype(jnp.float32)
+        lead = spread(lead_hl[g], 0) * dot(c_g, h_lead[g])
+        mixed = y_acc[g] + lead + skip_of(g) * xc[g].astype(jnp.float32)
         follow_copy(g).wait_recv()
-        mixed = mixed + dot(lead_hl[g], expand[1]) * dot(c_g, follow_in[g])
+        mixed = mixed + spread(lead_hl[g], 1) * dot(c_g, follow_in[g])
         gated = mixed * silu(gate_ref[:, wide].astype(jnp.float32))
         mean_sq = jnp.mean(gated * gated, axis=1, keepdims=True)
         token_out = (gated * lax.rsqrt(mean_sq + 1e-05) * gain_ref[:, wide]).astype(jnp.bfloat16)
@@ -293,13 +322,6 @@
     width = PER * HEADDIM
     vis = visit_span.shape[0]
 
-    def by_group(v):
-        v = v.reshape(2, tokens, groups, PER).transpose(2, 1, 0, 3).reshape(groups, tokens, 2 * PER)
-        return jnp.pad(v, ((0, 0), (0, 0), (0, 128 - 2 * PER)))
-
-    rate = by_group(log_decay * LOG2E - BIG * resets.astype(jnp.float32)[None, :, None])
-    log_weight = by_group(jnp.maximum(0.5 * jnp.log2(-jnp.expm1(2.0 * log_decay)), -1000.0))
-    spans = jnp.pad(visit_span, ((0, 0), (0, 126)))
     f32, bf16 = jnp.float32, jnp.bfloat16
     state = (groups, STATE, width)
     whole = pl.BlockSpec(memory_space=pltpu.VMEM)
@@ -315,14 +337,14 @@
         scratch_shapes=[
             pltpu.VMEM((HALO, channels), bf16),
             pltpu.VMEM((HALO, 2 * groups * STATE), bf16),
-            pltpu.VMEM((vis, 128), jnp.int32),
+            pltpu.VMEM((2, vis), jnp.int32),
             pltpu.VMEM((groups, tokens, width), bf16),
             pltpu.VMEM((groups, tokens, STATE), bf16),
             pltpu.VMEM((groups, tokens, STATE), bf16),
-            pltpu.VMEM((groups, tokens, 128), f32),
-            pltpu.VMEM((groups, 128, tokens), f32),
-            pltpu.VMEM((groups, tokens, 128), bf16),
-            pltpu.VMEM((2, 128, width), bf16),
+            pltpu.VMEM((groups, tokens, 2 * PER), f32),
+            pltpu.VMEM((groups, 2 * PER, tokens), f32),
+            pltpu.VMEM((groups, 4 * PER, tokens), bf16),
+            pltpu.VMEM((2, 4 * PER, width), bf16),
             pltpu.VMEM((groups, tokens, width), f32),
             pltpu.VMEM(state, bf16),
             pltpu.VMEM(state, f32),
@@ -341,19 +363,19 @@
             pair, pair, pair, pair, pair,
         ],
         compiler_params=pltpu.CompilerParams(
-            collective_id=0, has_side_effects=True, vmem_limit_bytes=60 << 20
+            collective_id=0, has_side_effects=True, vmem_limit_bytes=LIMIT << 20
         ),
     )(
         x_in,
         bc_in.reshape(tokens, 2 * groups * STATE),
         gate_z,
-        rate,
-        log_weight,
+        log_decay.transpose(0, 2, 1),
+        resets[None, :],
         conv_x,
-        conv_bc.reshape(4, 2 * groups * STATE),
-        jnp.repeat(skip_d, HEADDIM)[None, :],
+        conv_bc,
+        skip_d[None, :],
         norm_gain[None, :],
-        spans,
+        visit_span.T,
     )
 
 

time: 64 us -> 59.3 us (0.927)
  Pallas kernels: 50.4 us -> 46.8 us
  other arithmetic: 1.73 us -> 0 us
    unnamed x9 -> x21, local copies, waits for them, and re-layouts: 6.78 us -> 11.4 us
    pallas_call x1, Pallas kernels: 50.4 us -> 46.8 us  [on_device(): pl.pallas_call(functools.partial(kernel, lax.axis_size('ctx'), groups), o...]
    pad x3 -> x0, local copies, waits for them, and re-layouts: 2.3 us -> none  [the longest x2 1.69 us: by_group(): return jnp.pad(v, ((0, 0), (0, 0), (0, 128 - 2 * PER)))]
    max x1 -> x0, other arithmetic: 1.04 us -> none  [on_device(): jnp.maximum(0.5 * jnp.log2(-jnp.expm1(2.0 * log_decay)), -1000.0)]
    broadcast_in_dim x1 -> x0, local copies, waits for them, and re-layouts: 0.72 us -> none  [on_device(): jnp.repeat(skip_d, HEADDIM)[None, :]]
    another operation x1 -> x0, local copies, waits for them, and re-layouts: 0.69 us -> none  [on_device(): jnp.repeat(skip_d, HEADDIM)[None, :]]
    mul x1 -> x0, other arithmetic: 0.68 us -> none  [on_device(): BIG * resets.astype(jnp.float32)[None, :, None]]
where the time goes in v2:
time: 59.3 us; the launch traced here: 58.9 us
  Pallas kernels  46.8 us (79%)
  local copies, waits for them, and re-layouts  11.4 us (19%)
  between operations  0.66 us (1%)
    pallas_call x1, Pallas kernels, on_device(): pl.pallas_call(functools.partial(kernel, lax.axis_size('ctx'), groups), o...  46.8 us
    unnamed x21, local copies, waits for them, and re-layouts  11.4 us

profile of v2, /device:TPU:1, one launch (start us, length us, event | category | flops | bytes accessed | tf_op | source)
XLA Modules:
  0.0 58.9 jit_solution(11373214587775091085)
XLA Ops:
  0.6 1.1 %copy.12 = bf16[32,8,2,512]{3,1,2,0:T(8,128)(2,1)S(1)} copy(bf16[32,8,2,512]{3,2,1,0:T(2,128)(2,1)} %bitcast.13) | data formatting | bytes 1048576
  1.7 0.0 copy-start
  1.8 1.6 %copy-done = bf16[256,4096]{1,0:T(8,128)(2,1)S(1)} copy-done((bf16[256,4096]{1,0:T(8,128)(2,1)S(1)}, bf16[256,4096]{1,0:T(8,128)(2,1)}, u32[]{:S(2)}) %copy-start) | copy-done | bytes 2097176
  3.3 0.0 copy-start.1
  3.3 1.6 %copy-done.1 = bf16[256,4096]{1,0:T(8,128)(2,1)S(1)} copy-done((bf16[256,4096]{1,0:T(8,128)(2,1)S(1)}, bf16[256,4096]{1,0:T(8,128)(2,1)}, u32[]{:S(2)}) %copy-start.1) | copy-done | bytes 2097176
  4.9 0.0 copy-start.2
  4.9 0.9 %copy-done.2 = f32[2,256,64]{1,2,0:T(8,128)S(1)} copy-done((f32[2,256,64]{1,2,0:T(8,128)S(1)}, f32[2,256,64]{1,2,0:T(8,128)}, u32[]{:S(2)}) %copy-start.2) | copy-done | bytes 131096
  5.8 0.0 copy-start.3
  5.8 0.8 %copy-done.3 = f32[4,4096]{1,0:T(4,128)S(1)} copy-done((f32[4,4096]{1,0:T(4,128)S(1)}, f32[4,4096]{1,0:T(4,128)}, u32[]{:S(2)}) %copy-start.3) | copy-done | bytes 65560
  6.7 0.0 copy-start.4
  6.7 0.7 %copy-done.4 = f32[4,2,512]{2,1,0:T(2,128)S(1)} copy-done((f32[4,2,512]{2,1,0:T(2,128)S(1)}, f32[4,2,512]{2,1,0:T(2,128)}, u32[]{:S(2)}) %copy-start.4) | copy-done | bytes 16408
  7.4 0.0 copy-start.5
  7.4 0.7 %copy-done.5 = f32[4096]{0:T(1024)S(1)} copy-done((f32[4096]{0:T(1024)S(1)}, f32[4096]{0:T(1024)}, u32[]{:S(2)}) %copy-start.5) | copy-done | bytes 16408
  8.1 0.0 copy-start.6
  8.1 0.7 %copy-done.6 = s32[256]{0:T(256)S(1)} copy-done((s32[256]{0:T(256)S(1)}, s32[256]{0:T(256)}, u32[]{:S(2)}) %copy-start.6) | copy-done | bytes 1048
  8.8 0.0 copy-start.7
  8.8 0.7 %copy-done.7 = s32[16,2]{0,1:T(2,128)S(1)} copy-done((s32[16,2]{0,1:T(2,128)S(1)}, s32[16,2]{0,1:T(2,128)}, u32[]{:S(2)}) %copy-start.7) | copy-done | bytes 152
  9.5 0.0 copy-start.8
  9.5 0.7 %copy-done.8 = f32[64]{0:T(128)S(1)} copy-done((f32[64]{0:T(128)S(1)}, f32[64]{0:T(128)}, u32[]{:S(2)}) %copy-start.8) | copy-done | bytes 280
  10.1 46.8 %shard_map.113 = (bf16[256,4096]{1,0:T(8,128)(2,1)S(1)}, bf16[16,4096]{1,0:T(8,128)(2,1)S(1)}) custom-call(bf16[256,4096]{1,0:T(8,128)(2,1)S(1)} %copy-done, bf16[256,1024]{1,0:T(8,128)(2,1)S(1)} %bitcast.7, bf16[256,4096]{1,0:T(8,128)(2,1)S(1)} %copy-done.1, f32[2,64,256]{2,1,0:T(8,128)S(1)} %bitcast.8, s32[1,256]{1,0:T(1,128)S(1)} %bitcast.10, ...), custom_call_target="tpu_custom_call" | custom-call | tf_op jit(solution)/shard_map/pallas_call | solution.py:329
  56.9 1.3 %copy.15 = bf16[256,4096]{1,0:T(8,128)(2,1)} copy(bf16[256,4096]{1,0:T(8,128)(2,1)S(1)} %get-tuple-element.4) | data formatting | bytes 4194304
  58.2 0.7 %copy.16 = bf16[16,4096]{1,0:T(8,128)(2,1)} copy(bf16[16,4096]{1,0:T(8,128)(2,1)S(1)} %get-tuple-element.5) | data formatting | bytes 262144
Async XLA Ops:
  1.7 1.6 %copy-start = (bf16[256,4096]{1,0:T(8,128)(2,1)S(1)}, bf16[256,4096]{1,0:T(8,128)(2,1)}, u32[]{:S(2)}) copy-start(bf16[256,4096]{1,0:T(8,128)(2,1)} %x_ref.1) | copy-start | bytes 6291460
  3.3 1.6 %copy-start.1 = (bf16[256,4096]{1,0:T(8,128)(2,1)S(1)}, bf16[256,4096]{1,0:T(8,128)(2,1)}, u32[]{:S(2)}) copy-start(bf16[256,4096]{1,0:T(8,128)(2,1)} %gate_ref.1) | copy-start | bytes 6291460
  4.9 0.9 %copy-start.2 = (f32[2,256,64]{1,2,0:T(8,128)S(1)}, f32[2,256,64]{1,2,0:T(8,128)}, u32[]{:S(2)}) copy-start(f32[2,256,64]{1,2,0:T(8,128)} %param.13) | copy-start | bytes 393220
  5.8 0.8 %copy-start.3 = (f32[4,4096]{1,0:T(4,128)S(1)}, f32[4,4096]{1,0:T(4,128)}, u32[]{:S(2)}) copy-start(f32[4,4096]{1,0:T(4,128)} %taps_x.1) | copy-start | bytes 196612
  6.7 0.7 %copy-start.4 = (f32[4,2,512]{2,1,0:T(2,128)S(1)}, f32[4,2,512]{2,1,0:T(2,128)}, u32[]{:S(2)}) copy-start(f32[4,2,512]{2,1,0:T(2,128)} %taps_bc.1) | copy-start | bytes 49156
  7.4 0.7 %copy-start.5 = (f32[4096]{0:T(1024)S(1)}, f32[4096]{0:T(1024)}, u32[]{:S(2)}) copy-start(f32[4096]{0:T(1024)} %param.18) | copy-start | bytes 49156
  8.1 0.7 %copy-start.6 = (s32[256]{0:T(256)S(1)}, s32[256]{0:T(256)}, u32[]{:S(2)}) copy-start(s32[256]{0:T(256)} %param.14) | copy-start | bytes 3076
  8.8 0.7 %copy-start.7 = (s32[16,2]{0,1:T(2,128)S(1)}, s32[16,2]{0,1:T(2,128)}, u32[]{:S(2)}) copy-start(s32[16,2]{0,1:T(2,128)} %param.19) | copy-start | bytes 388
  9.5 0.7 %copy-start.8 = (f32[64]{0:T(128)S(1)}, f32[64]{0:T(128)}, u32[]{:S(2)}) copy-start(f32[64]{0:T(128)} %param.17) | copy-start | bytes 772

commit v3 on v2

--- a/solution.py
+++ b/solution.py
@@ -12,7 +12,7 @@
 PER = 16
 LOG2E = 1.4426950408889634
 BIG = 160.0
-LIMIT = 34
+LIMIT = 57
 HALO = 8
 MESH = pl.DeviceIdType.MESH
 
@@ -36,16 +36,19 @@
 def kernel(
     chips,
     groups,
+    x_hbm, bc_hbm, gate_hbm, rate_hbm, reset_hbm, taps_x_hbm, taps_bc_hbm, skip_hbm, gain_hbm, span_hbm,
+    out_ref, pool_ref,
     x_ref, bc_ref, gate_ref, rate_ref, reset_ref, taps_x, taps_bc, skip_ref, gain_ref, span_ref,
-    out_ref, pool_ref,
     halo_x, halo_bc, span_in, xc, bs, cs, colt, rowt, lead_hl, expand, y_acc, h_lead,
     s_own, t_own, s_send, t_send, s_in, t_in, chain_in, follow_in, chain_out,
     own_pool, spill_out, spill_in,
-    sem_halo, sem_s, sem_t, sem_chain, sem_follow, sem_spill,
+    sem_in, sem_halo, sem_s, sem_t, sem_chain, sem_follow, sem_spill,
 ):
     tokens = x_ref.shape[0]
     width = PER * HEADDIM
     half = tokens // 2
+    part = width // 2
+    chunks = 2 * groups
     c = lax.axis_index("ctx")
     d = lax.axis_index("dp")
     other = 1 - d
@@ -61,6 +64,12 @@
     spill_to = {"ctx": d * c + (1 - d) * nxt, "dp": other}
     follow_chain = {"ctx": nxt, "dp": d}
 
+    sources = (x_hbm, bc_hbm, rate_hbm, reset_hbm, taps_x_hbm, taps_bc_hbm, gate_hbm, skip_hbm, gain_hbm, span_hbm)
+    places = (x_ref, bc_ref, rate_ref, reset_ref, taps_x, taps_bc, gate_ref, skip_ref, gain_ref, span_ref)
+    loads = [pltpu.make_async_copy(sources[k], places[k], sem_in.at[k]) for k in range(10)]
+    for load in loads:
+        load.start()
+
     barrier = pltpu.get_barrier_semaphore()
     pl.semaphore_signal(barrier, inc=1, device_id=partner, device_id_type=MESH)
 
@@ -83,9 +92,9 @@
 
     tail = pl.ds(tokens - HALO, HALO)
     halos = (
-        remote(x_ref.at[tail], halo_x, sem_halo, 0, halo_to),
-        remote(bc_ref.at[tail], halo_bc, sem_halo, 1, halo_to),
-        remote(span_ref, span_in, sem_halo, 2, halo_to),
+        remote(x_hbm.at[tail], halo_x, sem_halo, 0, halo_to),
+        remote(bc_hbm.at[tail], halo_bc, sem_halo, 1, halo_to),
+        remote(span_hbm, span_in, sem_halo, 2, halo_to),
     )
 
     @pl.when(index < last_index)
@@ -116,6 +125,9 @@
     ehead = lax.div(lax.broadcasted_iota(jnp.int32, (4 * PER, width), 1), HEADDIM)
     expand[0] = (erow == ehead + PER * (1 - d)).astype(jnp.float32).astype(jnp.bfloat16)
     expand[1] = (erow == ehead + PER * d).astype(jnp.float32).astype(jnp.bfloat16)
+    for load in loads[:6]:
+        load.wait()
+
     fold = BIG * reset_ref[...].astype(jnp.float32)
 
     @pl.when(index == 0)
@@ -145,6 +157,27 @@
 
     def taps_of(ref, which, at):
         return [ref[k, which : which + 1, at] for k in range(4)]
+
+    def relay(g):
+        s_copy(g).wait_recv()
+        t_copy(g).wait_recv()
+
+        @pl.when(has_prev)
+        def _():
+            chain_copy(g).wait_recv()
+
+        @pl.when(pos == 0)
+        def _():
+            chain_in[g] = jnp.zeros_like(chain_in[g])
+
+        follow_copy(g).start()
+        state = t_in[g][0:1] * chain_in[g].astype(jnp.float32) + s_in[g].astype(jnp.float32)
+        h_lead[g] = state.astype(jnp.bfloat16)
+
+        @pl.when(has_next)
+        def _():
+            chain_out[g] = (t_own[g][0:1] * state + s_own[g]).astype(jnp.bfloat16)
+            chain_copy(g).start()
 
     @pl.loop(0, groups)
     def _(g):
@@ -174,36 +207,39 @@
         xc[g] = x_g
         xf = x_g.astype(jnp.float32)
         sent = (xf * spread(to_end, 1)).astype(jnp.bfloat16)
-        s_send[g] = lax.dot_general(b_g, sent, across, preferred_element_type=jnp.float32).astype(jnp.bfloat16)
-        t_send[g] = spread_end(total, 1)
-        s_copy(g).start()
-        t_copy(g).start()
+        state = lax.dot_general(b_g, sent, across, preferred_element_type=jnp.float32)
+        ends = spread_end(total, 1)
+        for k in range(2):
+            s_send[2 * g + k] = state[:, k * part : (k + 1) * part].astype(jnp.bfloat16)
+            t_send[2 * g + k] = ends[:, k * part : (k + 1) * part]
+            s_copy(2 * g + k).start()
+            t_copy(2 * g + k).start()
         kept = (xf * spread(to_end, 0)).astype(jnp.bfloat16)
-        s_own[g] = lax.dot_general(b_g, kept, across, preferred_element_type=jnp.float32)
-        t_own[g] = spread_end(total, 0)
-
-    def relay(g):
-        s_copy(g).wait_recv()
-        t_copy(g).wait_recv()
-
-        @pl.when(has_prev)
-        def _():
-            chain_copy(g).wait_recv()
-
-        @pl.when(pos == 0)
-        def _():
-            chain_in[g] = jnp.zeros_like(chain_in[g])
-
-        follow_copy(g).start()
-        state = t_in[g][0:1] * chain_in[g].astype(jnp.float32) + s_in[g].astype(jnp.float32)
-        h_lead[g] = state.astype(jnp.bfloat16)
-
-        @pl.when(has_next)
-        def _():
-            chain_out[g] = (t_own[g][0:1] * state + s_own[g]).astype(jnp.bfloat16)
-            chain_copy(g).start()
-
-    slots = 2 * groups
+        state = lax.dot_general(b_g, kept, across, preferred_element_type=jnp.float32)
+        ends = spread_end(total, 0)
+        for k in range(2):
+            s_own[2 * g + k] = state[:, k * part : (k + 1) * part]
+            t_own[2 * g + k] = ends[:, k * part : (k + 1) * part]
+
+        @pl.when((pos == 0) & (g > 0))
+        def _():
+            relay(2 * g - 2)
+            relay(2 * g - 1)
+
+    slots = 4 * groups
+    first = 7 * jnp.maximum(pos - 1, 0) - 4
+    done_early = jnp.where(pos == 0, chunks - 2, jnp.where(pos == 1, 2, 0))
+    done_before = jnp.where(pos == 0, chunks, jnp.clip(lax.div(slots - first + 2, 3), 0, chunks))
+
+    @pl.when(pos == 0)
+    def _():
+        relay(chunks - 2)
+        relay(chunks - 1)
+
+    @pl.when(pos == 1)
+    def _():
+        relay(0)
+        relay(1)
 
     left = lax.broadcasted_iota(jnp.int32, (tokens, 128), 1) < HEADDIM
     lower = rows[:half, :half] >= cols[:half, :half]
@@ -211,14 +247,14 @@
     @pl.loop(0, groups)
     def _(g):
         score = lax.dot_general(cs[g], bs[g], (((1,), (1,)), ((), ())), preferred_element_type=jnp.float32)
-        for part in range(2):
-            turn = 2 * g + part - 2 * pos
-
-            @pl.when((turn >= 0) & (turn < groups))
+        for quarter in range(4):
+            turn = 4 * g + quarter - first
+
+            @pl.when((pos > 0) & (turn >= 0) & (lax.rem(turn, 3) == 0) & (lax.div(turn, 3) >= done_early) & (lax.div(turn, 3) < chunks))
             def _():
-                relay(turn)
-
-            for pair in range(part * PER // 4, (part + 1) * PER // 4):
+                relay(lax.div(turn, 3))
+
+            for pair in range(quarter * PER // 8, (quarter + 1) * PER // 8):
                 at = pair * 2 * HEADDIM
                 x_pair = xc[g, :, at : at + 2 * HEADDIM]
                 got = []
@@ -238,6 +274,9 @@
                     got.append(dot(jnp.concatenate([mix_top, mix_bottom], axis=0), x_pair))
                 y_acc[g, :, at : at + 2 * HEADDIM] = jnp.where(left, got[0], got[1])
 
+    for load in loads[6:]:
+        load.wait()
+
     vis = span_ref.shape[1]
     token = index * tokens + lax.broadcasted_iota(jnp.int32, (tokens, vis), 0)
 
@@ -259,16 +298,24 @@
 
     @pl.loop(0, groups)
     def _(g):
-        @pl.when(g + 2 * pos >= slots)
-        def _():
-            relay(g)
+        begin = jnp.where(g == 0, done_before, jnp.clip(jnp.maximum(2 * g, done_before + 2 * g), 0, chunks))
+        finish = jnp.clip(done_before + 2 * g + 2, 0, chunks)
+
+        @pl.when(begin < finish)
+        def _():
+            relay(begin)
+
+        @pl.when(begin + 1 < finish)
+        def _():
+            relay(begin + 1)
 
         wide = pl.ds(pl.multiple_of(g * width, width), width)
         c_g = cs[g]
-        lead = spread(lead_hl[g], 0) * dot(c_g, h_lead[g])
+        lead = spread(lead_hl[g], 0) * dot(c_g, jnp.concatenate([h_lead[2 * g], h_lead[2 * g + 1]], axis=1))
         mixed = y_acc[g] + lead + skip_of(g) * xc[g].astype(jnp.float32)
-        follow_copy(g).wait_recv()
-        mixed = mixed + spread(lead_hl[g], 1) * dot(c_g, follow_in[g])
+        follow_copy(2 * g).wait_recv()
+        follow_copy(2 * g + 1).wait_recv()
+        mixed = mixed + spread(lead_hl[g], 1) * dot(c_g, jnp.concatenate([follow_in[2 * g], follow_in[2 * g + 1]], axis=1))
         gated = mixed * silu(gate_ref[:, wide].astype(jnp.float32))
         mean_sq = jnp.mean(gated * gated, axis=1, keepdims=True)
         token_out = (gated * lax.rsqrt(mean_sq + 1e-05) * gain_ref[:, wide]).astype(jnp.bfloat16)
@@ -294,18 +341,20 @@
         def _():
             pool_ref[:, wide] = (own_pool[g] / length).astype(jnp.bfloat16)
 
-    @pl.loop(0, groups)
-    def _(g):
-        s_copy(g).wait_send()
-        t_copy(g).wait_send()
-        follow_copy(g).wait_send()
+    @pl.loop(0, chunks)
+    def _(q):
+        s_copy(q).wait_send()
+        t_copy(q).wait_send()
+        follow_copy(q).wait_send()
 
         @pl.when(has_next)
         def _():
-            chain_copy(g).wait_send()
-
-        @pl.when(index > 0)
-        def _():
+            chain_copy(q).wait_send()
+
+    @pl.when(index > 0)
+    def _():
+        @pl.loop(0, groups)
+        def _(g):
             spill_copy(g).wait_send()
 
     @pl.when(index < last_index)
@@ -323,18 +372,33 @@
     vis = visit_span.shape[0]
 
     f32, bf16 = jnp.float32, jnp.bfloat16
-    state = (groups, STATE, width)
+    state = (2 * groups, STATE, width // 2)
+    ends = (2 * groups, 8, width // 2)
     whole = pl.BlockSpec(memory_space=pltpu.VMEM)
-    pair = pltpu.SemaphoreType.DMA((2, groups))
+    outside = pl.BlockSpec(memory_space=pltpu.HBM)
+    per_chunk = pltpu.SemaphoreType.DMA((2, 2 * groups))
+    operands = (
+        x_in,
+        bc_in.reshape(tokens, 2 * groups * STATE),
+        gate_z,
+        log_decay.transpose(0, 2, 1),
+        resets[None, :],
+        conv_x,
+        conv_bc,
+        skip_d[None, :],
+        norm_gain[None, :],
+        visit_span.T,
+    )
     return pl.pallas_call(
         functools.partial(kernel, lax.axis_size("ctx"), groups),
         out_shape=(
             jax.ShapeDtypeStruct((tokens, channels), bf16),
             jax.ShapeDtypeStruct((vis, channels), bf16),
         ),
-        in_specs=[whole] * 10,
+        in_specs=[outside] * 10,
         out_specs=(whole, whole),
         scratch_shapes=[
+            *(pltpu.VMEM(v.shape, v.dtype) for v in operands),
             pltpu.VMEM((HALO, channels), bf16),
             pltpu.VMEM((HALO, 2 * groups * STATE), bf16),
             pltpu.VMEM((2, vis), jnp.int32),
@@ -348,35 +412,26 @@
             pltpu.VMEM((groups, tokens, width), f32),
             pltpu.VMEM(state, bf16),
             pltpu.VMEM(state, f32),
-            pltpu.VMEM((groups, 8, width), f32),
-            pltpu.VMEM(state, bf16),
-            pltpu.VMEM((groups, 8, width), f32),
-            pltpu.VMEM(state, bf16),
-            pltpu.VMEM((groups, 8, width), f32),
+            pltpu.VMEM(ends, f32),
+            pltpu.VMEM(state, bf16),
+            pltpu.VMEM(ends, f32),
+            pltpu.VMEM(state, bf16),
+            pltpu.VMEM(ends, f32),
             pltpu.VMEM(state, bf16),
             pltpu.VMEM(state, bf16),
             pltpu.VMEM(state, bf16),
             pltpu.VMEM((groups, vis, width), f32),
             pltpu.VMEM((groups, vis, width), f32),
             pltpu.VMEM((groups, vis, width), f32),
+            pltpu.SemaphoreType.DMA((10,)),
             pltpu.SemaphoreType.DMA((2, 3)),
-            pair, pair, pair, pair, pair,
+            per_chunk, per_chunk, per_chunk, per_chunk,
+            pltpu.SemaphoreType.DMA((2, groups)),
         ],
         compiler_params=pltpu.CompilerParams(
             collective_id=0, has_side_effects=True, vmem_limit_bytes=LIMIT << 20
         ),
-    )(
-        x_in,
-        bc_in.reshape(tokens, 2 * groups * STATE),
-        gate_z,
-        log_decay.transpose(0, 2, 1),
-        resets[None, :],
-        conv_x,
-        conv_bc,
-        skip_d[None, :],
-        norm_gain[None, :],
-        visit_span.T,
-    )
+    )(*operands)
 
 
 def solution(mesh):

time: 59.3 us -> 48.9 us (0.82)
  local copies, waits for them, and re-layouts: 11.4 us -> 5.73 us
  Pallas kernels: 46.8 us -> 41.9 us
    unnamed x21 -> x5, local copies, waits for them, and re-layouts: 11.4 us -> 5.73 us
    pallas_call x1, Pallas kernels: 46.8 us -> 41.9 us  [on_device(): pl.pallas_call(functools.partial(kernel, lax.axis_size('ctx'), groups), o...]
where the time goes in v3:
time: 48.9 us; the launch traced here: 48.3 us
  Pallas kernels  41.9 us (86%)
  local copies, waits for them, and re-layouts  5.73 us (12%)
  between operations  0.65 us (1%)
    pallas_call x1, Pallas kernels, on_device(): pl.pallas_call(functools.partial(kernel, lax.axis_size('ctx'), groups), o...  41.9 us
    unnamed x5, local copies, waits for them, and re-layouts  5.73 us

profile of v3, /device:TPU:1, one launch (start us, length us, event | category | flops | bytes accessed | tf_op | source)
XLA Modules:
  0.0 48.3 jit_solution(6842693973667020017)
XLA Ops:
  0.6 1.9 %copy.12 = bf16[32,8,2,512]{3,1,2,0:T(8,128)(2,1)} copy(bf16[32,8,2,512]{3,2,1,0:T(2,128)(2,1)} %bitcast.8) | data formatting | bytes 1048576
  2.5 41.9 %shard_map.113 = (bf16[256,4096]{1,0:T(8,128)(2,1)}, bf16[16,4096]{1,0:T(8,128)(2,1)}) custom-call(bf16[256,4096]{1,0:T(8,128)(2,1)} %x_hbm.1, bf16[256,1024]{1,0:T(8,128)(2,1)} %bitcast.7, bf16[256,4096]{1,0:T(8,128)(2,1)} %gate_hbm.1, f32[2,64,256]{2,1,0:T(8,128)} %bitcast.9, s32[1,256]{1,0:T(1,128)} %bitcast.11, f32[4,4096]{1,0:T(4,128)} %taps_x_hbm.1, ...), custom_call_target="tpu_custom_call" | custom-call | tf_op jit(solution)/shard_map/pallas_call | solution.py:392
  44.5 0.0 copy-start
  44.5 3.2 %copy.15 = bf16[256,4096]{1,0:T(8,128)(2,1)} copy(bf16[256,4096]{1,0:T(8,128)(2,1)} %get-tuple-element.4) | data formatting | bytes 4194304
  47.7 0.0 copy-done
  47.7 0.7 %copy.16 = bf16[16,4096]{1,0:T(8,128)(2,1)} copy(bf16[16,4096]{1,0:T(8,128)(2,1)S(1)} %copy-done) | data formatting | bytes 262144
Async XLA Ops:
  44.5 3.2 %copy-start = (bf16[16,4096]{1,0:T(8,128)(2,1)S(1)}, bf16[16,4096]{1,0:T(8,128)(2,1)}, u32[]{:S(2)}) copy-start(bf16[16,4096]{1,0:T(8,128)(2,1)} %get-tuple-element.5) | copy-start | bytes 393220

commit v4 on v3

--- a/solution.py
+++ b/solution.py
@@ -37,12 +37,13 @@
     chips,
     groups,
     x_hbm, bc_hbm, gate_hbm, rate_hbm, reset_hbm, taps_x_hbm, taps_bc_hbm, skip_hbm, gain_hbm, span_hbm,
-    out_ref, pool_ref,
+    out_hbm, pool_ref,
+    out_ref,
     x_ref, bc_ref, gate_ref, rate_ref, reset_ref, taps_x, taps_bc, skip_ref, gain_ref, span_ref,
     halo_x, halo_bc, span_in, xc, bs, cs, colt, rowt, lead_hl, expand, y_acc, h_lead,
     s_own, t_own, s_send, t_send, s_in, t_in, chain_in, follow_in, chain_out,
     own_pool, spill_out, spill_in,
-    sem_in, sem_halo, sem_s, sem_t, sem_chain, sem_follow, sem_spill,
+    sem_in, sem_out, sem_halo, sem_s, sem_t, sem_chain, sem_follow, sem_spill,
 ):
     tokens = x_ref.shape[0]
     width = PER * HEADDIM
@@ -114,6 +115,10 @@
     def follow_copy(g):
         return remote(chain_in.at[g], follow_in.at[g], sem_follow, g, partner)
 
+    def out_copy(g):
+        at = pl.ds(pl.multiple_of(g * width, width), width)
+        return pltpu.make_async_copy(out_ref.at[:, at], out_hbm.at[:, at], sem_out.at[g])
+
     def spill_copy(g):
         return remote(spill_out.at[g], spill_in.at[g], sem_spill, g, spill_to)
 
@@ -170,14 +175,15 @@
         def _():
             chain_in[g] = jnp.zeros_like(chain_in[g])
 
-        follow_copy(g).start()
         state = t_in[g][0:1] * chain_in[g].astype(jnp.float32) + s_in[g].astype(jnp.float32)
-        h_lead[g] = state.astype(jnp.bfloat16)
 
         @pl.when(has_next)
         def _():
             chain_out[g] = (t_own[g][0:1] * state + s_own[g]).astype(jnp.bfloat16)
             chain_copy(g).start()
+
+        follow_copy(g).start()
+        h_lead[g] = state.astype(jnp.bfloat16)
 
     @pl.loop(0, groups)
     def _(g):
@@ -320,6 +326,7 @@
         mean_sq = jnp.mean(gated * gated, axis=1, keepdims=True)
         token_out = (gated * lax.rsqrt(mean_sq + 1e-05) * gain_ref[:, wide]).astype(jnp.bfloat16)
         out_ref[:, wide] = token_out
+        out_copy(g).start()
         sums = dot(inside, token_out)
         own_pool[g] = sums[:vis]
         spill_out[g] = sums[vis:]
@@ -340,6 +347,10 @@
         @pl.when(index == last_index)
         def _():
             pool_ref[:, wide] = (own_pool[g] / length).astype(jnp.bfloat16)
+
+    @pl.loop(0, groups)
+    def _(g):
+        out_copy(g).wait()
 
     @pl.loop(0, chunks)
     def _(q):
@@ -396,8 +407,9 @@
             jax.ShapeDtypeStruct((vis, channels), bf16),
         ),
         in_specs=[outside] * 10,
-        out_specs=(whole, whole),
+        out_specs=(outside, whole),
         scratch_shapes=[
+            pltpu.VMEM((tokens, channels), bf16),
             *(pltpu.VMEM(v.shape, v.dtype) for v in operands),
             pltpu.VMEM((HALO, channels), bf16),
             pltpu.VMEM((HALO, 2 * groups * STATE), bf16),
@@ -424,6 +436,7 @@
             pltpu.VMEM((groups, vis, width), f32),
             pltpu.VMEM((groups, vis, width), f32),
             pltpu.SemaphoreType.DMA((10,)),
+            pltpu.SemaphoreType.DMA((groups,)),
             pltpu.SemaphoreType.DMA((2, 3)),
             per_chunk, per_chunk, per_chunk, per_chunk,
             pltpu.SemaphoreType.DMA((2, groups)),

time: 48.9 us -> 49 us (level)
  the two profiles are of different devices: /device:TPU:1 before, /device:TPU:0 now
where the time goes in v4:
time: 49 us; the launch traced here: 48.8 us
  Pallas kernels  42.4 us (87%)
  local copies, waits for them, and re-layouts  5.73 us (12%)
  between operations  0.65 us (1%)
    pallas_call x1, Pallas kernels, on_device(): pl.pallas_call(functools.partial(kernel, lax.axis_size('ctx'), groups), o...  42.4 us
    unnamed x5, local copies, waits for them, and re-layouts  5.73 us

profile of v4, /device:TPU:0, one launch (start us, length us, event | category | flops | bytes accessed | tf_op | source)
XLA Modules:
  0.0 48.8 jit_solution(4456215278220657449)
XLA Ops:
  0.6 1.9 %copy.12 = bf16[32,8,2,512]{3,1,2,0:T(8,128)(2,1)} copy(bf16[32,8,2,512]{3,2,1,0:T(2,128)(2,1)} %bitcast.8) | data formatting | bytes 1048576
  2.5 42.4 %shard_map.113 = (bf16[256,4096]{1,0:T(8,128)(2,1)}, bf16[16,4096]{1,0:T(8,128)(2,1)}) custom-call(bf16[256,4096]{1,0:T(8,128)(2,1)} %x_hbm.1, bf16[256,1024]{1,0:T(8,128)(2,1)} %bitcast.7, bf16[256,4096]{1,0:T(8,128)(2,1)} %gate_hbm.1, f32[2,64,256]{2,1,0:T(8,128)} %bitcast.9, s32[1,256]{1,0:T(1,128)} %bitcast.11, f32[4,4096]{1,0:T(4,128)} %taps_x_hbm.1, ...), custom_call_target="tpu_custom_call" | custom-call | tf_op jit(solution)/shard_map/pallas_call | solution.py:403
  44.9 0.0 copy-start
  44.9 3.2 %copy.15 = bf16[256,4096]{1,0:T(8,128)(2,1)} copy(bf16[256,4096]{1,0:T(8,128)(2,1)} %get-tuple-element.4) | data formatting | bytes 4194304
  48.1 0.0 copy-done
  48.1 0.7 %copy.16 = bf16[16,4096]{1,0:T(8,128)(2,1)} copy(bf16[16,4096]{1,0:T(8,128)(2,1)S(1)} %copy-done) | data formatting | bytes 262144
Async XLA Ops:
  44.9 3.2 %copy-start = (bf16[16,4096]{1,0:T(8,128)(2,1)S(1)}, bf16[16,4096]{1,0:T(8,128)(2,1)}, u32[]{:S(2)}) copy-start(bf16[16,4096]{1,0:T(8,128)(2,1)} %get-tuple-element.5) | copy-start | bytes 393220
